TPU v7x, 128 devices: a whole 4x4x4 slice. The times are simulated.
128 devices in a mesh: wide: 8 (over z, x_lo), narrow: 16 (over y, x_hi, core).
Axes of the slice: x: 4 (x_hi: 2, x_lo: 2; x = x_hi * 2 + x_lo), y: 4, z: 4, core: 2. Of those that a mesh axis runs over, the one named last changes fastest.
Arguments:
- samples: bfloat16 [1024, 2, 102144], P(('wide', 'narrow')), may hold values from -6 to 6
- filter_taps: float32 [16, 256], replicated, may hold values from -1.5 to 1.5
- beam_weights: bfloat16 [256, 2, 2, 512, 1024], P(('narrow', 'wide')), may hold values from -0.1875 to 0.1875
- smooth_kernel: float32 [33, 33], replicated, may hold values from -0.1875 to 0.1875
Outputs:
- detection: float32 [256, 48, 1024], P('narrow', None, 'wide')
All inputs are finite; a program needn't handle non-finite values.
Results may differ from a plain program's by a relative error of at most 0.012.
The roundings to bfloat16 on the way count: a program that leaves them out, or rounds other values in their place, can miss the bound.
Values may be sent and summed in bfloat16 or wider, within the bound.
No kernel may reach another device: no remote copies, remote signals or barrier semaphores. Data moves between devices by JAX's collectives and lax.ppermute only.
A program may use at most 256 MiB of HBM per device.

v0:
```python
import functools

import jax
import jax.numpy as jnp
import ml_dtypes
import numpy as np
from jax import lax
from jax.experimental import pallas as pl
from jax.experimental.pallas import tpu as pltpu
from jax.sharding import PartitionSpec as P

INTEG = 8
HALF = 16
LANES = 128
PASSES = 3


def fourier_table(points, wide_count, narrow_count):
    per_device = points // (wide_count * narrow_count)
    slot = np.arange(wide_count * narrow_count)
    first = (slot % narrow_count * wide_count + slot // narrow_count) * per_device
    channel = (first[:, None] + np.arange(per_device)[None, :]).reshape(-1)
    angle = (channel[:, None] * np.arange(points)[None, :] % points) * (2.0 * np.pi / points)
    cosine = np.cos(angle) / np.sqrt(points)
    sine = np.sin(angle) / np.sqrt(points)
    real_row = np.stack([cosine, sine], axis=1)
    imag_row = np.stack([-sine, cosine], axis=1)
    table = np.stack([real_row, imag_row], axis=1)
    halves = points // LANES
    table = table.reshape(points, 2, 2, halves, LANES).transpose(0, 1, 3, 2, 4)
    table = table.reshape(2 * points, 2 * points).astype(np.float32)
    high = table.astype(ml_dtypes.bfloat16)
    low = (table - high.astype(np.float32)).astype(ml_dtypes.bfloat16)
    return high, low


def channelize_kernel(
    frames, spectra, tap_count, group, x_ref, taps_ref, high_ref, low_ref, out_ref, flat, windowed, turned
):
    step = pl.program_id(0)
    bins = spectra // INTEG
    rows = x_ref.shape[0] // group
    per_frame = rows // frames
    flat[...] = x_ref[...].astype(jnp.float32)
    for member in range(group):
        for part in range(per_frame):
            taps = [taps_ref[part // 2, tap] for tap in range(tap_count)]
            for chunk in range(bins // 8):
                totals = [None] * INTEG
                for shift in range(INTEG + tap_count - 1):
                    start = member * rows + per_frame * (shift + chunk * 8 * INTEG) + part
                    values = flat[pl.ds(start, 8, stride=per_frame * INTEG), :]
                    for phase in range(max(0, shift - tap_count + 1), min(INTEG, shift + 1)):
                        term = taps[shift - phase] * values
                        totals[phase] = term if totals[phase] is None else totals[phase] + term
                for phase in range(INTEG):
                    row = member * spectra + phase * bins + chunk * 8
                    windowed[row : row + 8, part * LANES : (part + 1) * LANES] = totals[phase]
    contract = (((1,), (1,)), ((), ()))
    exact = windowed[...]
    high = exact.astype(jnp.bfloat16)
    spectrum = lax.dot_general(high_ref[...], high, contract, preferred_element_type=jnp.float32)
    if PASSES > 1:
        low = (exact - high.astype(jnp.float32)).astype(jnp.bfloat16)
        spectrum += lax.dot_general(high_ref[...], low, contract, preferred_element_type=jnp.float32)
    if PASSES > 2:
        spectrum += lax.dot_general(low_ref[...], high, contract, preferred_element_type=jnp.float32)
    outputs = high_ref.shape[0]
    inputs_here = turned.shape[1] // outputs
    for member in range(group):
        for column in range(spectra // LANES):
            start = member * spectra + column * LANES
            turned[column, pl.ds(step * group + member, outputs, stride=inputs_here), :] = spectrum[
                :, start : start + LANES
            ]

    @pl.when(step == pl.num_programs(0) - 1)
    def _():
        for column in range(spectra // LANES):
            out_ref[:, column * LANES : (column + 1) * LANES] = turned[column].astype(jnp.bfloat16)


def channelize(samples, filter_taps, wide_count, narrow_count):
    inputs_here, _, length = samples.shape
    tap_count, points = filter_taps.shape
    frames = length // points
    spectra = frames - tap_count + 1
    halves = points // LANES
    group = 2
    high, low = fourier_table(points, wide_count, narrow_count)
    lined = samples.reshape(inputs_here, 2, frames, halves, LANES).transpose(0, 2, 3, 1, 4)
    lined = lined.reshape(-1, LANES)
    taps = filter_taps.reshape(tap_count, halves, 1, LANES).transpose(1, 0, 2, 3)
    taps = jnp.broadcast_to(taps, (halves, tap_count, 8, LANES))
    rows = lined.shape[0] // inputs_here * group
    owners = wide_count * narrow_count
    whole = lambda array: pl.BlockSpec(array.shape, lambda i: (0,) * array.ndim)
    voltage = pl.pallas_call(
        functools.partial(channelize_kernel, frames, spectra, tap_count, group),
        out_shape=jax.ShapeDtypeStruct((2 * points * inputs_here, spectra), jnp.bfloat16),
        grid=(inputs_here // group,),
        in_specs=[
            pl.BlockSpec((rows, LANES), lambda i: (i, 0)),
            whole(taps),
            whole(high),
            whole(low),
        ],
        out_specs=pl.BlockSpec((2 * points * inputs_here, spectra), lambda i: (0, 0)),
        scratch_shapes=[
            pltpu.VMEM((rows, LANES), jnp.float32),
            pltpu.VMEM((group * spectra, 2 * points), jnp.float32),
            pltpu.VMEM((spectra // LANES, 2 * points * inputs_here, LANES), jnp.float32),
        ],
        compiler_params=pltpu.CompilerParams(vmem_limit_bytes=40 << 20),
        name="channelize",
    )(lined, taps, jnp.asarray(high), jnp.asarray(low))
    return voltage.reshape(owners, points // owners, 2, inputs_here, spectra)


def beam_kernel(scale, volt_ref, weight_ref, out_ref, total):
    pol = pl.program_id(1)
    sources, _, _, inputs, spectra = volt_ref.shape
    dishes = sources * inputs
    bins = spectra // INTEG
    real = volt_ref[:, 0, 0].reshape(dishes, spectra).T
    imag = volt_ref[:, 0, 1].reshape(dishes, spectra).T
    lhs = jnp.concatenate(
        [jnp.concatenate([real, -imag], axis=1), jnp.concatenate([imag, real], axis=1)], axis=0
    )
    beams = weight_ref.shape[-1]
    width = 256
    for block in range(beams // width):
        columns = slice(block * width, (block + 1) * width)
        weights = weight_ref[0, 0, :, :, columns].reshape(2 * dishes, width)
        formed = jnp.dot(lhs, weights, preferred_element_type=jnp.float32)
        power = formed * formed
        power = power[:spectra] + power[spectra:]
        binned = power[0:bins]
        for phase in range(1, INTEG):
            binned = binned + power[phase * bins : (phase + 1) * bins]

        @pl.when(pol == 0)
        def _():
            total[:, columns] = binned

        @pl.when(pol > 0)
        def _():
            total[:, columns] += binned

    @pl.when(pol == pl.num_programs(1) - 1)
    def _():
        chunk = out_ref.shape[-1]
        for owner in range(out_ref.shape[0]):
            values = total[:, owner * chunk : (owner + 1) * chunk] * jnp.float32(scale)
            out_ref[owner, 0] = values.astype(jnp.bfloat16)


def beam_power(turned, beam_weights, wide_count):
    sources, per_device, _, inputs, spectra = turned.shape
    pols, dishes, beams = beam_weights.shape[1], beam_weights.shape[3], beam_weights.shape[4]
    bins = spectra // INTEG
    return pl.pallas_call(
        functools.partial(beam_kernel, 1.0 / (pols * INTEG)),
        out_shape=jax.ShapeDtypeStruct((wide_count, per_device, bins, beams // wide_count), jnp.bfloat16),
        grid=(per_device, pols),
        in_specs=[
            pl.BlockSpec((sources // pols, 1, 2, inputs, spectra), lambda c, p: (p, c, 0, 0, 0)),
            pl.BlockSpec((1, 1, 2, dishes, beams), lambda c, p: (c, p, 0, 0, 0)),
        ],
        out_specs=pl.BlockSpec((wide_count, 1, bins, beams // wide_count), lambda c, p: (0, c, 0, 0)),
        scratch_shapes=[pltpu.VMEM((bins, beams), jnp.float32)],
        compiler_params=pltpu.CompilerParams(vmem_limit_bytes=40 << 20),
        name="beam_power",
    )(turned, beam_weights)


def banded(smooth_kernel, channels_here, bins):
    extent = smooth_kernel.shape[0]
    half = extent // 2
    positions = jnp.arange(bins, dtype=jnp.int32)
    distance = positions[None, :] - positions[:, None] + half
    selector = (distance[None] == jnp.arange(extent, dtype=jnp.int32)[:, None, None]).astype(jnp.bfloat16)
    toeplitz = jnp.einsum(
        "dtu,kd->tku", selector, smooth_kernel.astype(jnp.bfloat16), preferred_element_type=jnp.float32
    ).astype(jnp.bfloat16)
    row = toeplitz.reshape(bins, extent * bins)
    shifted = [
        jnp.pad(row, ((0, 0), (c * bins, (channels_here - 1 - c) * bins))) for c in range(channels_here)
    ]
    return jnp.concatenate(shifted, axis=0)


def smooth_body(low_ref, mid_ref, high_ref, matrix_ref, out_ref):
    channels, bins, beams = mid_ref.shape
    centered = []
    for ref in (low_ref, mid_ref, high_ref):
        values = ref[...].astype(jnp.float32)
        values = values - jnp.mean(values, axis=1, keepdims=True)
        centered.append(values.astype(jnp.bfloat16).reshape(channels * bins, beams))
    stacked = jnp.concatenate(centered, axis=0)
    result = jnp.dot(matrix_ref[...], stacked, preferred_element_type=jnp.float32)
    out_ref[...] = result.reshape(channels, bins, beams)


def smooth(low, mid, high, matrix):
    vmem = pl.BlockSpec(memory_space=pltpu.VMEM)
    return pl.pallas_call(
        smooth_body,
        out_shape=jax.ShapeDtypeStruct(mid.shape, jnp.float32),
        in_specs=[vmem] * 4,
        out_specs=vmem,
        compiler_params=pltpu.CompilerParams(vmem_limit_bytes=40 << 20),
        name="smooth",
    )(low, mid, high, matrix)


def body(samples, filter_taps, beam_weights, smooth_kernel):
    wide_count = lax.axis_size("wide")
    narrow_count = lax.axis_size("narrow")
    voltage = channelize(samples, filter_taps, wide_count, narrow_count)
    voltage, smooth_kernel = lax.optimization_barrier((voltage, smooth_kernel))
    turned = lax.all_to_all(voltage, ("wide", "narrow"), split_axis=0, concat_axis=0, tiled=True)
    intensity = beam_power(turned, beam_weights, wide_count)
    bins, beams = intensity.shape[2], intensity.shape[3]
    by_beam = lax.all_to_all(intensity, "wide", split_axis=0, concat_axis=0, tiled=True)
    by_beam = by_beam.reshape(-1, bins, beams)
    forward = [(i, i + 1) for i in range(narrow_count - 1)]
    backward = [(target, source) for source, target in forward]
    low = lax.ppermute(by_beam, "narrow", forward)
    high = lax.ppermute(by_beam, "narrow", backward)
    return smooth(low, by_beam, high, banded(smooth_kernel, by_beam.shape[0], bins))


def solution(mesh):
    placed = (
        P(("wide", "narrow"), None, None),
        P(),
        P(("narrow", "wide"), None, None, None, None),
        P(),
    )
    return jax.shard_map(
        body, mesh=mesh, in_specs=placed, out_specs=P("narrow", None, "wide"), check_vma=False
    )
```

profile of v0, /device:TPU:8, one launch (start us, length us, event | category | flops | bytes accessed | tf_op | source)
XLA Modules:
  0.0 125.3 jit_solution(5209657874842570864)
XLA Ops:
  0.0 0.7 reshape.33
  0.8 0.0 copy-start.1
  0.8 1.9 %copy-done.1 = bf16[8,2,102144]{2,1,0:T(2,128)(2,1)S(1)} copy-done((bf16[8,2,102144]{2,1,0:T(2,128)(2,1)S(1)}, bf16[8,2,102144]{2,1,0:T(2,128)(2,1)}, u32[]{:S(2)}) %copy-start.1) | copy-done | bytes 3268632
  2.7 0.0 copy-start.2
  2.7 1.0 copy-done.2
  3.7 0.0 copy-start.3
  3.7 1.0 copy-done.3
  4.8 23.0 %channelize.1 = bf16[4096,384]{1,0:T(8,128)(2,1)} custom-call(bf16[12768,128]{1,0:T(8,128)(2,1)S(1)} %bitcast.17, f32[2,16,8,128]{3,2,1,0:T(8,128)S(1)} %broadcast_in_dim.5.taps_ref, bf16[512,512]{1,0:T(8,128)(2,1)S(1)} %copy-done.3, bf16[512,512]{1,0:T(8,128)(2,1)S(1)} %copy-done.2), custom_call_target="tpu_custom_call" | custom-call | tf_op jit(solution)/shard_map/channelize/pallas_call | solution.py:98
  27.8 0.0 copy-start.4
  27.8 10.4 %all-to-all-start = ((bf16[128,2,2,8,384]{4,3,2,1,0:T(8,128)(2,1)}), bf16[128,2,2,8,384]{4,3,2,1,0:T(8,128)(2,1)S(1)}, u32[]{:S(2)}, u32[]{:S(2)}) async-start(bf16[128,2,2,8,384]{4,3,2,1,0:T(8,128)(2,1)} %bitcast.5), calls=%async_computation | async-start | bytes 6291456 | tf_op jit(solution)/shard_map/all_to_all | solution.py:222
  38.3 0.0 copy-done.4
  38.3 1.1 fusion
  39.4 1.4 %reshape.36 = bf16[48,1584]{1,0:T(8,128)(2,1)S(1)} reshape(bf16[48,33,48]{2,1,0:T(8,128)(2,1)} %fusion) | data formatting | bytes 304128 | tf_op jit(solution)/shard_map/reshape | solution.py:186
  40.7 0.7 pad_dynamic-update-slice_fusion.15
  41.4 0.8 pad_dynamic-update-slice_fusion.14
  42.2 0.8 pad_dynamic-update-slice_fusion.13
  43.0 0.8 pad_dynamic-update-slice_fusion.12
  43.9 0.8 pad_dynamic-update-slice_fusion.11
  44.7 0.8 pad_dynamic-update-slice_fusion.10
  45.5 0.8 pad_dynamic-update-slice_fusion.9
  46.3 0.8 pad_dynamic-update-slice_fusion.8
  47.1 0.7 pad_dynamic-update-slice_fusion.7
  47.8 0.8 pad_dynamic-update-slice_fusion.6
  48.6 0.8 pad_dynamic-update-slice_fusion.5
  49.4 0.8 pad_dynamic-update-slice_fusion.4
  50.2 0.8 pad_dynamic-update-slice_fusion.3
  51.0 0.8 pad_dynamic-update-slice_fusion.2
  51.8 26.4 %all-to-all-done.volt_ref = bf16[128,2,2,8,384]{4,3,2,1,0:T(8,128)(2,1)S(1)} async-done(((bf16[128,2,2,8,384]{4,3,2,1,0:T(8,128)(2,1)}), bf16[128,2,2,8,384]{4,3,2,1,0:T(8,128)(2,1)S(1)}, u32[]{:S(2)}, u32[]{:S(2)}) %all-to-all-start) | async-done | bytes 3145760 | tf_op jit(solution)/shard_map/all_to_all | solution.py:222
  78.3 0.0 copy-start
  78.3 3.4 %copy-done = bf16[2,2,2,512,1024]{4,3,2,1,0:T(8,128)(2,1)S(1)} copy-done((bf16[2,2,2,512,1024]{4,3,2,1,0:T(8,128)(2,1)S(1)}, bf16[2,2,2,512,1024]{4,3,2,1,0:T(8,128)(2,1)}, u32[]{:S(2)}) %copy-start) | copy-done | bytes 8388632
  81.7 16.7 %beam_power.1 = bf16[8,2,48,128]{3,2,1,0:T(8,128)(2,1)} custom-call(bf16[128,2,2,8,384]{4,3,2,1,0:T(8,128)(2,1)S(1)} %all-to-all-done.volt_ref, bf16[2,2,2,512,1024]{4,3,2,1,0:T(8,128)(2,1)S(1)} %copy-done), custom_call_target="tpu_custom_call" | custom-call | tf_op jit(solution)/shard_map/beam_power/pallas_call | solution.py:162
  98.4 3.4 %all-to-all-start.1 = ((bf16[8,2,48,128]{3,2,1,0:T(8,128)(2,1)}), bf16[8,2,48,128]{3,2,1,0:T(8,128)(2,1)S(1)}, u32[]{:S(2)}, u32[]{:S(2)}) async-start(bf16[8,2,48,128]{3,2,1,0:T(8,128)(2,1)} %beam_power.1), calls=%async_computation.1 | async-start | bytes 393216 | tf_op jit(solution)/shard_map/all_to_all | solution.py:225
  101.8 0.8 pad_dynamic-update-slice_fusion.1
  102.6 6.1 %all-to-all-done.1 = bf16[8,2,48,128]{3,2,1,0:T(8,128)(2,1)S(1)} async-done(((bf16[8,2,48,128]{3,2,1,0:T(8,128)(2,1)}), bf16[8,2,48,128]{3,2,1,0:T(8,128)(2,1)S(1)}, u32[]{:S(2)}, u32[]{:S(2)}) %all-to-all-start.1) | async-done | bytes 196640 | tf_op jit(solution)/shard_map/all_to_all | solution.py:225
  108.6 3.4 %collective-permute-start.1 = (bf16[16,48,128]{2,1,0:T(8,128)(2,1)S(1)}, bf16[16,48,128]{2,1,0:T(8,128)(2,1)S(1)}, u32[]{:S(2)}, u32[]{:S(2)}) collective-permute-start(bf16[16,48,128]{2,1,0:T(8,128)(2,1)S(1)} %bitcast.18), channel_id=1, source_target_pairs={{1,0},{2,1},{3,2},{4,3},{5,4},{6,5},{7,6},{8,7},{9,8},{10,9},{11,1... | collective-permute-start | bytes 589832 | tf_op jit(solution)/shard_map/ppermute | solution.py:230
  112.1 1.9 %collective-permute-start = (bf16[16,48,128]{2,1,0:T(8,128)(2,1)S(1)}, bf16[16,48,128]{2,1,0:T(8,128)(2,1)S(1)}, u32[]{:S(2)}, u32[]{:S(2)}) collective-permute-start(bf16[16,48,128]{2,1,0:T(8,128)(2,1)S(1)} %bitcast.19), channel_id=1, source_target_pairs={{0,1},{1,2},{2,3},{3,4},{4,5},{5,6},{6,7},{7,8},{8,9},{9,10},{10,1... | collective-permute-start | bytes 589832 | tf_op jit(solution)/shard_map/ppermute | solution.py:229
  114.0 0.8 pad_dynamic-update-slice_fusion.matrix_ref
  114.8 0.5 collective-permute-done.1.high_ref
  115.3 6.1 %collective-permute-done.low_ref = bf16[16,48,128]{2,1,0:T(8,128)(2,1)S(1)} collective-permute-done((bf16[16,48,128]{2,1,0:T(8,128)(2,1)S(1)}, bf16[16,48,128]{2,1,0:T(8,128)(2,1)S(1)}, u32[]{:S(2)}, u32[]{:S(2)}) %collective-permute-start) | collective-permute-done | bytes 196640 | tf_op jit(solution)/shard_map/ppermute | solution.py:229
  121.5 3.9 %smooth.1 = f32[16,48,128]{2,1,0:T(8,128)} custom-call(bf16[16,48,128]{2,1,0:T(8,128)(2,1)S(1)} %collective-permute-done.low_ref, bf16[16,48,128]{2,1,0:T(8,128)(2,1)S(1)} %bitcast.20, bf16[16,48,128]{2,1,0:T(8,128)(2,1)S(1)} %collective-permute-done.1.high_ref, bf16[768,2304]{1,0:T(8,128)(2,1)} %pad_dynamic-update-slice_fusion.matrix_ref), custom_call_target="tpu_custom_call" | custom-call | tf_op jit(solution)/shard_map/smooth/pallas_call | solution.py:207
  (3 shorter events, 0.0 us)
Async XLA Ops:
  0.8 1.9 %copy-start.1 = (bf16[8,2,102144]{2,1,0:T(2,128)(2,1)S(1)}, bf16[8,2,102144]{2,1,0:T(2,128)(2,1)}, u32[]{:S(2)}) copy-start(bf16[8,2,102144]{2,1,0:T(2,128)(2,1)} %param.6) | copy-start | bytes 9805828
  2.7 1.0 copy-start.2
  3.7 1.0 copy-start.3
  27.8 10.5 %copy-start.4 = (f32[33,33]{1,0:T(8,128)S(1)}, f32[33,33]{1,0:T(8,128)}, u32[]{:S(2)}) copy-start(f32[33,33]{1,0:T(8,128)} %param.9) | copy-start | bytes 13072
  27.8 50.5 %all-to-all-start = ((bf16[128,2,2,8,384]{4,3,2,1,0:T(8,128)(2,1)}), bf16[128,2,2,8,384]{4,3,2,1,0:T(8,128)(2,1)S(1)}, u32[]{:S(2)}, u32[]{:S(2)}) async-start(bf16[128,2,2,8,384]{4,3,2,1,0:T(8,128)(2,1)} %bitcast.5), calls=%async_computation | async-start | bytes 6291456 | tf_op jit(solution)/shard_map/all_to_all | solution.py:222
  78.3 3.4 %copy-start = (bf16[2,2,2,512,1024]{4,3,2,1,0:T(8,128)(2,1)S(1)}, bf16[2,2,2,512,1024]{4,3,2,1,0:T(8,128)(2,1)}, u32[]{:S(2)}) copy-start(bf16[2,2,2,512,1024]{4,3,2,1,0:T(8,128)(2,1)} %weight_ref.1) | copy-start | bytes 25165828
  98.4 10.3 %all-to-all-start.1 = ((bf16[8,2,48,128]{3,2,1,0:T(8,128)(2,1)}), bf16[8,2,48,128]{3,2,1,0:T(8,128)(2,1)S(1)}, u32[]{:S(2)}, u32[]{:S(2)}) async-start(bf16[8,2,48,128]{3,2,1,0:T(8,128)(2,1)} %beam_power.1), calls=%async_computation.1 | async-start | bytes 393216 | tf_op jit(solution)/shard_map/all_to_all | solution.py:225
  108.6 6.7 %collective-permute-start.1 = (bf16[16,48,128]{2,1,0:T(8,128)(2,1)S(1)}, bf16[16,48,128]{2,1,0:T(8,128)(2,1)S(1)}, u32[]{:S(2)}, u32[]{:S(2)}) collective-permute-start(bf16[16,48,128]{2,1,0:T(8,128)(2,1)S(1)} %bitcast.18), channel_id=1, source_target_pairs={{1,0},{2,1},{3,2},{4,3},{5,4},{6,5},{7,6},{8,7},{9,8},{10,9},{11,1... | collective-permute-start | bytes 589832 | tf_op jit(solution)/shard_map/ppermute | solution.py:230
  112.1 9.4 %collective-permute-start = (bf16[16,48,128]{2,1,0:T(8,128)(2,1)S(1)}, bf16[16,48,128]{2,1,0:T(8,128)(2,1)S(1)}, u32[]{:S(2)}, u32[]{:S(2)}) collective-permute-start(bf16[16,48,128]{2,1,0:T(8,128)(2,1)S(1)} %bitcast.19), channel_id=1, source_target_pairs={{0,1},{1,2},{2,3},{3,4},{4,5},{5,6},{6,7},{7,8},{8,9},{9,10},{10,1... | collective-permute-start | bytes 589832 | tf_op jit(solution)/shard_map/ppermute | solution.py:229
where the time goes:
time: 126 us; the launch traced here: 125 us
  Pallas kernels  43.6 us (35%)
  waiting for transfers between devices  39.2 us (31%)
  local copies, waits for them, and re-layouts  22.2 us (18%)
  starting transfers between devices  19.2 us (15%)
    all_to_all x1, waiting for transfers between devices, body(): lax.all_to_all(voltage, ('wide', 'narrow'), split_axis=0, concat_axis=0,...  26.4 us
    pallas_call x1, Pallas kernels, channelize(): pl.pallas_call(functools.partial(channelize_kernel, frames, spectra, tap_...  23 us
    unnamed x25, local copies, waits for them, and re-layouts  19.3 us
    pallas_call x1, Pallas kernels, beam_power(): pl.pallas_call(functools.partial(beam_kernel, 1.0 / (pols * INTEG)), out_...  16.7 us
    all_to_all x1, starting transfers between devices, body(): lax.all_to_all(voltage, ('wide', 'narrow'), split_axis=0, concat_axis=0,...  10.4 us
    ppermute x1, waiting for transfers between devices, body(): low = lax.ppermute(by_beam, 'narrow', forward)  6.14 us
    all_to_all x1, waiting for transfers between devices, body(): lax.all_to_all(intensity, 'wide', split_axis=0, concat_axis=0, tiled=True)  6.08 us
    pallas_call x1, Pallas kernels, smooth(): pl.pallas_call(smooth_body, out_shape=jax.ShapeDtypeStruct(mid.shape, jnp...  3.86 us
  transfers between devices with their start and end apart: 4, of which 4 were waited for; matrix products, arithmetic and copies ran while one was open for 12% of the time, Pallas kernels for 0%

commit v1 on v0

v1 whole, which is shorter than its diff:
```python
import functools

import jax
import jax.numpy as jnp
import ml_dtypes
import numpy as np
from jax import lax
from jax.experimental import pallas as pl
from jax.experimental.pallas import tpu as pltpu
from jax.sharding import PartitionSpec as P

INTEG = 8
HALF = 16
LANES = 128


def fourier_table(points, wide_count, narrow_count):
    per_device = points // (wide_count * narrow_count)
    slot = np.arange(wide_count * narrow_count)
    first = (slot % narrow_count * wide_count + slot // narrow_count) * per_device
    channel = (first[:, None] + np.arange(per_device)[None, :]).reshape(-1)
    angle = (channel[:, None] * np.arange(points)[None, :] % points) * (2.0 * np.pi / points)
    cosine = np.cos(angle) / np.sqrt(points)
    sine = np.sin(angle) / np.sqrt(points)
    real_row = np.stack([cosine, sine], axis=1)
    imag_row = np.stack([-sine, cosine], axis=1)
    table = np.stack([real_row, imag_row], axis=1)
    halves = points // LANES
    table = table.reshape(points, 2, 2, halves, LANES).transpose(0, 1, 3, 2, 4)
    table = table.reshape(2 * points, 2 * points).astype(np.float32)
    high = table.astype(ml_dtypes.bfloat16)
    low = (table - high.astype(np.float32)).astype(ml_dtypes.bfloat16)
    return high, low


def channelize_kernel(
    frames, spectra, tap_count, group, x_ref, taps_ref, high_ref, out_ref, lined, windowed, turned
):
    step = pl.program_id(0)
    rows = x_ref.shape[0] // group
    per_frame = rows // frames
    segment = spectra // 8
    span = segment * per_frame
    needed = (segment + tap_count - 1) * per_frame
    pitch = lined.shape[0] // group
    half_taps = tap_count // 2
    pairs = segment // 2

    for member in range(group):
        for lane in range(8):
            count = min(-(-needed // 8) * 8, rows - lane * span)
            start = member * rows + lane * span
            values = x_ref[start : start + count, :].astype(jnp.float32)
            lined[pl.ds(member * pitch + lane, count, stride=8), :] = values

    def window(member, part):
        half = part // 2
        columns = slice(half * LANES, (half + 1) * LANES)
        taps = [jnp.broadcast_to(taps_ref[t : t + 1, columns], (8, LANES)) for t in range(tap_count)]
        even, odd = taps[0::2], taps[1::2]
        both = [first + second for first, second in zip(even, odd)]

        def frame(index):
            start = member * pitch + (per_frame * index + part) * 8
            return lined[start : start + 8, :]

        def put(index, values):
            row = member * spectra + index * 8
            windowed[row : row + 8, part * LANES : (part + 1) * LANES] = values

        def feed(totals, factors, values, index, count):
            for tap in range(half_taps):
                target = index - tap
                if 0 <= target < count:
                    term = factors[tap] * values
                    totals[target] = totals[target] + term if target in totals else term

        evens, odds, sums = {}, {}, {}
        late = None
        for index in range(pairs + half_taps):
            early = frame(2 * index)
            feed(evens, even, early, index, pairs + 1)
            if index > 0:
                feed(odds, odd, late, index - 1, pairs)
                feed(sums, both, late + early, index - 1, pairs)
                done = index - half_taps
                if done >= 0:
                    second = odds.pop(done)
                    put(2 * done, evens[done] + second)
                    put(2 * done + 1, sums.pop(done) - (evens[done + 1] + second))
                    evens.pop(done)
            if index < pairs + half_taps - 1:
                late = frame(2 * index + 1)

    contract = (((1,), (1,)), ((), ()))
    outputs = high_ref.shape[0]
    inputs_here = turned.shape[1] // outputs
    for member in range(group):
        for part in range(per_frame):
            window(member, part)
        high = windowed[member * spectra : (member + 1) * spectra, :].astype(jnp.bfloat16)
        spectrum = lax.dot_general(high_ref[...], high, contract, preferred_element_type=jnp.float32)
        for column in range(spectra // LANES):
            turned[column, pl.ds(step * group + member, outputs, stride=inputs_here), :] = spectrum[
                :, column * LANES : (column + 1) * LANES
            ]

    @pl.when(step == pl.num_programs(0) - 1)
    def _():
        for column in range(spectra // LANES):
            out_ref[:, column * LANES : (column + 1) * LANES] = turned[column].astype(jnp.bfloat16)


def channelize(samples, filter_taps, wide_count, narrow_count):
    inputs_here, _, length = samples.shape
    tap_count, points = filter_taps.shape
    frames = length // points
    spectra = frames - tap_count + 1
    halves = points // LANES
    group = 4
    high, _ = fourier_table(points, wide_count, narrow_count)
    lined = samples.reshape(inputs_here, 2, frames, halves, LANES).transpose(0, 2, 3, 1, 4)
    lined = lined.reshape(-1, LANES)
    rows = lined.shape[0] // inputs_here * group
    owners = wide_count * narrow_count
    pitch = -(-(spectra // 8 + tap_count - 1) * 2 * halves // 8) * 64
    whole = lambda array: pl.BlockSpec(array.shape, lambda i: (0,) * array.ndim)
    voltage = pl.pallas_call(
        functools.partial(channelize_kernel, frames, spectra, tap_count, group),
        out_shape=jax.ShapeDtypeStruct((2 * points * inputs_here, spectra), jnp.bfloat16),
        grid=(inputs_here // group,),
        in_specs=[
            pl.BlockSpec((rows, LANES), lambda i: (i, 0)),
            whole(filter_taps),
            whole(high),
        ],
        out_specs=pl.BlockSpec((2 * points * inputs_here, spectra), lambda i: (0, 0)),
        scratch_shapes=[
            pltpu.VMEM((group * pitch, LANES), jnp.float32),
            pltpu.VMEM((group * spectra, 2 * points), jnp.float32),
            pltpu.VMEM((spectra // LANES, 2 * points * inputs_here, LANES), jnp.float32),
        ],
        compiler_params=pltpu.CompilerParams(vmem_limit_bytes=60 << 20),
        name="channelize",
    )(lined, filter_taps, jnp.asarray(high))
    return voltage.reshape(owners, points // owners, 2, inputs_here, spectra)


def beam_kernel(scale, volt_ref, weight_ref, out_ref, held, arrived):
    sources, per_device, _, inputs, spectra = volt_ref.shape
    pols, beams = weight_ref.shape[1], weight_ref.shape[-1]
    each = sources // pols
    dishes = each * inputs
    owners, chunk = out_ref.shape[0], out_ref.shape[-1]
    copies = {}
    for channel in range(per_device):
        for pol in range(pols):
            copies[channel, pol] = pltpu.make_async_copy(
                weight_ref.at[channel, pol], held.at[channel, pol], arrived.at[channel, pol]
            )
            copies[channel, pol].start()
    for channel in range(per_device):
        total = None
        for pol in range(pols):
            rows = slice(pol * each, (pol + 1) * each)
            real = volt_ref[rows, channel, 0].reshape(dishes, spectra).T
            imag = volt_ref[rows, channel, 1].reshape(dishes, spectra).T
            lhs = jnp.concatenate(
                [jnp.concatenate([real, -imag], axis=1), jnp.concatenate([imag, real], axis=1)], axis=0
            )
            copies[channel, pol].wait()
            weights = held[channel, pol].reshape(2 * dishes, beams)
            formed = jnp.dot(lhs, weights, preferred_element_type=jnp.float32)
            power = formed * formed
            power = power[:spectra] + power[spectra:]
            power = power.reshape(spectra // (8 * INTEG), INTEG, 8, beams).sum(axis=1)
            total = power if total is None else total + power
        total = (total.reshape(spectra // INTEG, beams) * jnp.float32(scale)).astype(jnp.bfloat16)
        for owner in range(owners):
            out_ref[owner, channel] = total[:, owner * chunk : (owner + 1) * chunk]


def beam_power(turned, weights, wide_count):
    per_device, spectra = turned.shape[1], turned.shape[4]
    pols, beams = weights.shape[1], weights.shape[4]
    bins = spectra // INTEG
    vmem = pl.BlockSpec(memory_space=pltpu.VMEM)
    return pl.pallas_call(
        functools.partial(beam_kernel, 1.0 / (pols * INTEG)),
        out_shape=jax.ShapeDtypeStruct((wide_count, per_device, bins, beams // wide_count), jnp.bfloat16),
        in_specs=[vmem, pl.BlockSpec(memory_space=pl.ANY)],
        out_specs=vmem,
        scratch_shapes=[
            pltpu.VMEM(weights.shape, weights.dtype),
            pltpu.SemaphoreType.DMA((per_device, pols)),
        ],
        compiler_params=pltpu.CompilerParams(vmem_limit_bytes=50 << 20),
        name="beam_power",
    )(turned, weights)


def band_kernel(row_ref, out_ref):
    bins, width = row_ref.shape
    for channel in range(out_ref.shape[0] // bins):
        shifted = pltpu.roll(row_ref[...], channel * bins, axis=1)
        out_ref[channel * bins : (channel + 1) * bins, :] = shifted.astype(jnp.bfloat16)


def banded(smooth_kernel, channels_here, bins):
    extent = smooth_kernel.shape[0]
    half = extent // 2
    stored = np.arange(bins) // 8 + np.arange(bins) % 8 * (bins // 8)
    distance = stored[None, :] - np.arange(bins)[:, None] + half
    selector = (distance[None] == np.arange(extent)[:, None, None]).astype(ml_dtypes.bfloat16)
    row = jnp.einsum(
        "dtu,kd->tku",
        jnp.asarray(selector),
        smooth_kernel.astype(jnp.bfloat16),
        preferred_element_type=jnp.float32,
    ).reshape(bins, extent * bins)
    width = (channels_here + extent - 1) * bins
    row = jnp.pad(row, ((0, 0), (0, width - extent * bins)))
    vmem = pl.BlockSpec(memory_space=pltpu.VMEM)
    return pl.pallas_call(
        band_kernel,
        out_shape=jax.ShapeDtypeStruct((channels_here * bins, width), jnp.bfloat16),
        in_specs=[vmem],
        out_specs=vmem,
        compiler_params=pltpu.CompilerParams(vmem_limit_bytes=16 << 20),
        name="band",
    )(row)


def smooth_body(low_ref, mid_ref, high_ref, matrix_ref, out_ref):
    channels, bins, beams = mid_ref.shape
    centered = []
    for ref in (low_ref, mid_ref, high_ref):
        values = ref[...].astype(jnp.float32)
        values = values - jnp.mean(values, axis=1, keepdims=True)
        centered.append(values.astype(jnp.bfloat16).reshape(channels * bins, beams))
    stacked = jnp.concatenate(centered, axis=0)
    result = jnp.dot(matrix_ref[...], stacked, preferred_element_type=jnp.float32)
    out_ref[...] = result.reshape(channels, bins, beams)


def smooth(low, mid, high, matrix):
    vmem = pl.BlockSpec(memory_space=pltpu.VMEM)
    return pl.pallas_call(
        smooth_body,
        out_shape=jax.ShapeDtypeStruct(mid.shape, jnp.float32),
        in_specs=[vmem] * 4,
        out_specs=vmem,
        compiler_params=pltpu.CompilerParams(vmem_limit_bytes=16 << 20),
        name="smooth",
    )(low, mid, high, matrix)


def body(samples, filter_taps, beam_weights, smooth_kernel):
    wide_count = lax.axis_size("wide")
    narrow_count = lax.axis_size("narrow")
    voltage = channelize(samples, filter_taps, wide_count, narrow_count)
    voltage, smooth_kernel = lax.optimization_barrier((voltage, smooth_kernel))
    turned = lax.all_to_all(voltage, ("wide", "narrow"), split_axis=0, concat_axis=0, tiled=True)
    per_device, spectra = turned.shape[1], turned.shape[4]
    matrix = banded(smooth_kernel, per_device * wide_count, spectra // INTEG)
    turned, matrix = lax.optimization_barrier((turned, matrix))
    intensity = beam_power(turned, beam_weights, wide_count)
    bins, beams = intensity.shape[2], intensity.shape[3]
    by_beam = lax.all_to_all(intensity, "wide", split_axis=0, concat_axis=0, tiled=True)
    by_beam = by_beam.reshape(-1, bins, beams)
    forward = [(i, i + 1) for i in range(narrow_count - 1)]
    backward = [(target, source) for source, target in forward]
    low = lax.ppermute(by_beam, "narrow", forward)
    high = lax.ppermute(by_beam, "narrow", backward)
    return smooth(low, by_beam, high, matrix)


def solution(mesh):
    placed = (
        P(("wide", "narrow"), None, None),
        P(),
        P(("narrow", "wide"), None, None, None, None),
        P(),
    )
    return jax.shard_map(
        body, mesh=mesh, in_specs=placed, out_specs=P("narrow", None, "wide"), check_vma=False
    )
```

time: 126 us -> 98.9 us (0.78)
  local copies, waits for them, and re-layouts: 22.2 us -> 0.3 us
  Pallas kernels: 43.6 us -> 26.5 us
  blocking collectives: 0 us -> 9.57 us
  waiting for transfers between devices: 39.2 us -> 45.7 us
  starting transfers between devices: 19.2 us -> 16.3 us
    unnamed x25 -> x4, local copies, waits for them, and re-layouts: 19.3 us -> 0.01 us
    all_to_all x1, waiting for transfers between devices: 26.4 us -> 38.2 us  [body(): lax.all_to_all(voltage, ('wide', 'narrow'), split_axis=0, concat_axis=0,...]
    pallas_call x1, Pallas kernels: 23 us -> 13 us  [channelize(): pl.pallas_call(functools.partial(channelize_kernel, frames, spectra, tap_...]
    all_to_all x0 -> x1, blocking collectives: none -> 9.57 us  [body(): lax.all_to_all(intensity, 'wide', split_axis=0, concat_axis=0, tiled=True)]
    all_to_all x1 -> x0, waiting for transfers between devices: 6.08 us -> none  [body(): lax.all_to_all(intensity, 'wide', split_axis=0, concat_axis=0, tiled=True)]
    pallas_call x1, Pallas kernels: 16.7 us -> 10.7 us  [beam_power(): pl.pallas_call(functools.partial(beam_kernel, 1.0 / (pols * INTEG)), out_...]
    all_to_all x1 -> x0, starting transfers between devices: 3.39 us -> none  [body(): lax.all_to_all(intensity, 'wide', split_axis=0, concat_axis=0, tiled=True)]
    pallas_call x1, Pallas kernels: 3.86 us -> 1.85 us  [smooth(): pl.pallas_call(smooth_body, out_shape=jax.ShapeDtypeStruct(mid.shape, jnp...]
  transfers between devices with their start and end apart: 4 -> 3, of which waited for: 4 -> 3; matrix products, arithmetic and copies ran while one was open for 12% -> 1% of each run, Pallas kernels for 0% -> 1%
where the time goes in v1:
time: 98.9 us; the launch traced here: 98.7 us
  waiting for transfers between devices  45.7 us (46%)
  Pallas kernels  26.5 us (27%)
  starting transfers between devices  16.3 us (16%)
  blocking collectives  9.57 us (10%)
    all_to_all x1, waiting for transfers between devices, body(): lax.all_to_all(voltage, ('wide', 'narrow'), split_axis=0, concat_axis=0,...  38.2 us
    pallas_call x1, Pallas kernels, channelize(): pl.pallas_call(functools.partial(channelize_kernel, frames, spectra, tap_...  13 us
    all_to_all x1, starting transfers between devices, body(): lax.all_to_all(voltage, ('wide', 'narrow'), split_axis=0, concat_axis=0,...  10.8 us
    pallas_call x1, Pallas kernels, beam_power(): pl.pallas_call(functools.partial(beam_kernel, 1.0 / (pols * INTEG)), out_...  10.7 us
    all_to_all x1, blocking collectives, body(): lax.all_to_all(intensity, 'wide', split_axis=0, concat_axis=0, tiled=True)  9.57 us
    ppermute x1, waiting for transfers between devices, body(): low = lax.ppermute(by_beam, 'narrow', forward)  5.95 us
    ppermute x1, starting transfers between devices, body(): high = lax.ppermute(by_beam, 'narrow', backward)  3.49 us
  transfers between devices with their start and end apart: 3, of which 3 were waited for; matrix products, arithmetic and copies ran while one was open for 1% of the time, Pallas kernels for 1%

profile of v1, /device:TPU:8, one launch (start us, length us, event | category | flops | bytes accessed | tf_op | source)
XLA Modules:
  0.0 98.7 jit_solution(15820253845747032634)
XLA Ops:
  0.0 13.0 %channelize.1 = bf16[4096,384]{1,0:T(8,128)(2,1)} custom-call(bf16[12768,128]{1,0:T(8,128)(2,1)} %bitcast.17, f32[16,256]{1,0:T(8,128)} %taps_ref.1, bf16[512,512]{1,0:T(8,128)(2,1)} %constant.7.clone.high_ref), custom_call_target="tpu_custom_call" | custom-call | tf_op jit(solution)/shard_map/channelize/pallas_call | solution.py:128
  13.0 0.0 copy-start
  13.0 0.0 copy-start.1
  13.0 10.8 %all-to-all-start = ((bf16[128,2,2,8,384]{4,3,2,1,0:T(8,128)(2,1)}), bf16[128,2,2,8,384]{4,3,2,1,0:T(8,128)(2,1)}, u32[]{:S(2)}, u32[]{:S(2)}) async-start(bf16[128,2,2,8,384]{4,3,2,1,0:T(8,128)(2,1)} %bitcast.16), calls=%async_computation | async-start | bytes 6291456 | tf_op jit(solution)/shard_map/all_to_all | solution.py:263
  23.9 0.0 copy-done
  23.9 0.0 copy-done.1
  23.9 0.3 convolution_bitcast_fusion
  24.2 0.3 reshape.18
  24.5 0.9 band.1.matrix_ref
  25.4 38.2 %all-to-all-done.volt_ref = bf16[128,2,2,8,384]{4,3,2,1,0:T(8,128)(2,1)} async-done(((bf16[128,2,2,8,384]{4,3,2,1,0:T(8,128)(2,1)}), bf16[128,2,2,8,384]{4,3,2,1,0:T(8,128)(2,1)}, u32[]{:S(2)}, u32[]{:S(2)}) %all-to-all-start) | async-done | bytes 3145760 | tf_op jit(solution)/shard_map/all_to_all | solution.py:263
  63.6 10.7 %beam_power.1 = bf16[8,2,48,128]{3,2,1,0:T(8,128)(2,1)S(1)} custom-call(bf16[128,2,2,8,384]{4,3,2,1,0:T(8,128)(2,1)} %all-to-all-done.volt_ref, bf16[2,2,2,512,1024]{4,3,2,1,0:T(8,128)(2,1)} %weight_ref.1), custom_call_target="tpu_custom_call" | custom-call | tf_op jit(solution)/shard_map/beam_power/pallas_call | solution.py:188
  74.3 9.6 %all_to_all.10 = bf16[8,2,48,128]{3,2,1,0:T(8,128)(2,1)S(1)} all-to-all(bf16[8,2,48,128]{3,2,1,0:T(8,128)(2,1)S(1)} %beam_power.1), channel_id=1, replica_groups=mesh['wide'=8,'narrow'=16] {'wide'}, dimensions={0} | all-to-all | bytes 393216 | tf_op jit(solution)/shard_map/all_to_all | solution.py:269
  83.9 3.5 %collective-permute-start.1 = (bf16[16,48,128]{2,1,0:T(8,128)(2,1)S(1)}, bf16[16,48,128]{2,1,0:T(8,128)(2,1)S(1)}, u32[]{:S(2)}, u32[]{:S(2)}) collective-permute-start(bf16[16,48,128]{2,1,0:T(8,128)(2,1)S(1)} %bitcast.13), channel_id=1, source_target_pairs={{1,0},{2,1},{3,2},{4,3},{5,4},{6,5},{7,6},{8,7},{9,8},{10,9},{11,1... | collective-permute-start | bytes 589832 | tf_op jit(solution)/shard_map/ppermute | solution.py:274
  87.4 1.9 %collective-permute-start = (bf16[16,48,128]{2,1,0:T(8,128)(2,1)S(1)}, bf16[16,48,128]{2,1,0:T(8,128)(2,1)S(1)}, u32[]{:S(2)}, u32[]{:S(2)}) collective-permute-start(bf16[16,48,128]{2,1,0:T(8,128)(2,1)S(1)} %bitcast.14), channel_id=1, source_target_pairs={{0,1},{1,2},{2,3},{3,4},{4,5},{5,6},{6,7},{7,8},{8,9},{9,10},{10,1... | collective-permute-start | bytes 589832 | tf_op jit(solution)/shard_map/ppermute | solution.py:273
  89.3 1.5 %collective-permute-done.1.high_ref = bf16[16,48,128]{2,1,0:T(8,128)(2,1)S(1)} collective-permute-done((bf16[16,48,128]{2,1,0:T(8,128)(2,1)S(1)}, bf16[16,48,128]{2,1,0:T(8,128)(2,1)S(1)}, u32[]{:S(2)}, u32[]{:S(2)}) %collective-permute-start.1) | collective-permute-done | bytes 196640 | tf_op jit(solution)/shard_map/ppermute | solution.py:274
  90.9 5.9 %collective-permute-done.low_ref = bf16[16,48,128]{2,1,0:T(8,128)(2,1)S(1)} collective-permute-done((bf16[16,48,128]{2,1,0:T(8,128)(2,1)S(1)}, bf16[16,48,128]{2,1,0:T(8,128)(2,1)S(1)}, u32[]{:S(2)}, u32[]{:S(2)}) %collective-permute-start) | collective-permute-done | bytes 196640 | tf_op jit(solution)/shard_map/ppermute | solution.py:273
  96.8 1.8 %smooth.1 = f32[16,48,128]{2,1,0:T(8,128)} custom-call(bf16[16,48,128]{2,1,0:T(8,128)(2,1)S(1)} %collective-permute-done.low_ref, bf16[16,48,128]{2,1,0:T(8,128)(2,1)S(1)} %bitcast.15, bf16[16,48,128]{2,1,0:T(8,128)(2,1)S(1)} %collective-permute-done.1.high_ref, bf16[768,2304]{1,0:T(8,128)(2,1)S(1)} %band.1.matrix_ref), custom_call_target="tpu_custom_call" | custom-call | tf_op jit(solution)/shard_map/smooth/pallas_call | solution.py:248
  (1 shorter events, 0.0 us)
Async XLA Ops:
  13.0 10.9 %copy-start = (bf16[33,48,48]{2,0,1:T(8,128)(2,1)S(1)}, bf16[33,48,48]{2,0,1:T(8,128)(2,1)}, u32[]{:S(2)}) copy-start(bf16[33,48,48]{2,0,1:T(8,128)(2,1)} %constant.8.clone) | copy-start | bytes 456196
  13.0 10.9 %copy-start.1 = (f32[33,33]{1,0:T(8,128)S(1)}, f32[33,33]{1,0:T(8,128)}, u32[]{:S(2)}) copy-start(f32[33,33]{1,0:T(8,128)} %param.9) | copy-start | bytes 13072
  13.0 50.6 %all-to-all-start = ((bf16[128,2,2,8,384]{4,3,2,1,0:T(8,128)(2,1)}), bf16[128,2,2,8,384]{4,3,2,1,0:T(8,128)(2,1)}, u32[]{:S(2)}, u32[]{:S(2)}) async-start(bf16[128,2,2,8,384]{4,3,2,1,0:T(8,128)(2,1)} %bitcast.16), calls=%async_computation | async-start | bytes 6291456 | tf_op jit(solution)/shard_map/all_to_all | solution.py:263
  83.9 6.9 %collective-permute-start.1 = (bf16[16,48,128]{2,1,0:T(8,128)(2,1)S(1)}, bf16[16,48,128]{2,1,0:T(8,128)(2,1)S(1)}, u32[]{:S(2)}, u32[]{:S(2)}) collective-permute-start(bf16[16,48,128]{2,1,0:T(8,128)(2,1)S(1)} %bitcast.13), channel_id=1, source_target_pairs={{1,0},{2,1},{3,2},{4,3},{5,4},{6,5},{7,6},{8,7},{9,8},{10,9},{11,1... | collective-permute-start | bytes 589832 | tf_op jit(solution)/shard_map/ppermute | solution.py:274
  87.4 9.4 %collective-permute-start = (bf16[16,48,128]{2,1,0:T(8,128)(2,1)S(1)}, bf16[16,48,128]{2,1,0:T(8,128)(2,1)S(1)}, u32[]{:S(2)}, u32[]{:S(2)}) collective-permute-start(bf16[16,48,128]{2,1,0:T(8,128)(2,1)S(1)} %bitcast.14), channel_id=1, source_target_pairs={{0,1},{1,2},{2,3},{3,4},{4,5},{5,6},{6,7},{7,8},{8,9},{9,10},{10,1... | collective-permute-start | bytes 589832 | tf_op jit(solution)/shard_map/ppermute | solution.py:273

commit v2 on v1

--- a/solution.py
+++ b/solution.py
@@ -12,29 +12,28 @@
 INTEG = 8
 HALF = 16
 LANES = 128
+BATCH = 2
 
 
 def fourier_table(points, wide_count, narrow_count):
     per_device = points // (wide_count * narrow_count)
     slot = np.arange(wide_count * narrow_count)
     first = (slot % narrow_count * wide_count + slot // narrow_count) * per_device
-    channel = (first[:, None] + np.arange(per_device)[None, :]).reshape(-1)
-    angle = (channel[:, None] * np.arange(points)[None, :] % points) * (2.0 * np.pi / points)
+    channel = first[None, :] + np.arange(per_device)[:, None]
+    angle = (channel[:, :, None] * np.arange(points // 2) % points) * (2.0 * np.pi / points)
     cosine = np.cos(angle) / np.sqrt(points)
     sine = np.sin(angle) / np.sqrt(points)
-    real_row = np.stack([cosine, sine], axis=1)
-    imag_row = np.stack([-sine, cosine], axis=1)
-    table = np.stack([real_row, imag_row], axis=1)
-    halves = points // LANES
-    table = table.reshape(points, 2, 2, halves, LANES).transpose(0, 1, 3, 2, 4)
-    table = table.reshape(2 * points, 2 * points).astype(np.float32)
+    real_row = np.concatenate([cosine, sine], axis=2)
+    imag_row = np.concatenate([-sine, cosine], axis=2)
+    table = np.stack([real_row, imag_row], axis=2).reshape(per_device, -1, points)
+    table = table.astype(np.float32)
     high = table.astype(ml_dtypes.bfloat16)
     low = (table - high.astype(np.float32)).astype(ml_dtypes.bfloat16)
-    return high, low
+    return np.concatenate([high, high, low], axis=2)
 
 
 def channelize_kernel(
-    frames, spectra, tap_count, group, x_ref, taps_ref, high_ref, out_ref, lined, windowed, turned
+    frames, spectra, tap_count, group, x_ref, taps_ref, table_ref, out_ref, lined, windowed, turned
 ):
     step = pl.program_id(0)
     rows = x_ref.shape[0] // group
@@ -93,22 +92,42 @@
                 late = frame(2 * index + 1)
 
     contract = (((1,), (1,)), ((), ()))
-    outputs = high_ref.shape[0]
-    inputs_here = turned.shape[1] // outputs
-    for member in range(group):
-        for part in range(per_frame):
-            window(member, part)
-        high = windowed[member * spectra : (member + 1) * spectra, :].astype(jnp.bfloat16)
-        spectrum = lax.dot_general(high_ref[...], high, contract, preferred_element_type=jnp.float32)
-        for column in range(spectra // LANES):
-            turned[column, pl.ds(step * group + member, outputs, stride=inputs_here), :] = spectrum[
-                :, column * LANES : (column + 1) * LANES
-            ]
+    parities, outputs, points = table_ref.shape[0], table_ref.shape[1], windowed.shape[1]
+    inputs_here = turned.shape[1] // (parities * outputs)
+    batch = BATCH
+    for first in range(0, group, batch):
+        for member in range(first, first + batch):
+            for part in range(per_frame):
+                window(member, part)
+        rows = slice(first * spectra, (first + batch) * spectra)
+        near = windowed[rows, : points // 2]
+        far = windowed[rows, points // 2 :]
+        for parity in range(parities):
+            folded = near + far if parity == 0 else near - far
+            high = folded.astype(jnp.bfloat16)
+            low = (folded - high.astype(jnp.float32)).astype(jnp.bfloat16)
+            spectrum = lax.dot_general(
+                table_ref[parity],
+                jnp.concatenate([high, low, high], axis=1),
+                contract,
+                preferred_element_type=jnp.float32,
+            )
+            for member in range(batch):
+                start = parity * outputs * inputs_here + step * group + first + member
+                for column in range(spectra // LANES):
+                    left = member * spectra + column * LANES
+                    turned[column, pl.ds(start, outputs, stride=inputs_here), :] = spectrum[
+                        :, left : left + LANES
+                    ]
 
     @pl.when(step == pl.num_programs(0) - 1)
     def _():
         for column in range(spectra // LANES):
-            out_ref[:, column * LANES : (column + 1) * LANES] = turned[column].astype(jnp.bfloat16)
+            columns = slice(column * LANES, (column + 1) * LANES)
+            for parity in range(parities):
+                count = outputs * inputs_here
+                values = turned[column, parity * count : (parity + 1) * count, :].astype(jnp.bfloat16)
+                out_ref[:, parity, :, columns] = values.reshape(out_ref.shape[0], -1, LANES)
 
 
 def channelize(samples, filter_taps, wide_count, narrow_count):
@@ -118,23 +137,24 @@
     spectra = frames - tap_count + 1
     halves = points // LANES
     group = 4
-    high, _ = fourier_table(points, wide_count, narrow_count)
+    table = fourier_table(points, wide_count, narrow_count)
     lined = samples.reshape(inputs_here, 2, frames, halves, LANES).transpose(0, 2, 3, 1, 4)
     lined = lined.reshape(-1, LANES)
     rows = lined.shape[0] // inputs_here * group
     owners = wide_count * narrow_count
+    shape = (owners, points // owners, 2 * inputs_here, spectra)
     pitch = -(-(spectra // 8 + tap_count - 1) * 2 * halves // 8) * 64
     whole = lambda array: pl.BlockSpec(array.shape, lambda i: (0,) * array.ndim)
     voltage = pl.pallas_call(
         functools.partial(channelize_kernel, frames, spectra, tap_count, group),
-        out_shape=jax.ShapeDtypeStruct((2 * points * inputs_here, spectra), jnp.bfloat16),
+        out_shape=jax.ShapeDtypeStruct(shape, jnp.bfloat16),
         grid=(inputs_here // group,),
         in_specs=[
             pl.BlockSpec((rows, LANES), lambda i: (i, 0)),
             whole(filter_taps),
-            whole(high),
+            whole(table),
         ],
-        out_specs=pl.BlockSpec((2 * points * inputs_here, spectra), lambda i: (0, 0)),
+        out_specs=pl.BlockSpec(shape, lambda i: (0, 0, 0, 0)),
         scratch_shapes=[
             pltpu.VMEM((group * pitch, LANES), jnp.float32),
             pltpu.VMEM((group * spectra, 2 * points), jnp.float32),
@@ -142,7 +162,7 @@
         ],
         compiler_params=pltpu.CompilerParams(vmem_limit_bytes=60 << 20),
         name="channelize",
-    )(lined, filter_taps, jnp.asarray(high))
+    )(lined, filter_taps, jnp.asarray(table))
     return voltage.reshape(owners, points // owners, 2, inputs_here, spectra)
 
 
@@ -199,14 +219,20 @@
     )(turned, weights)
 
 
-def band_kernel(row_ref, out_ref):
+def band_kernel(odd_ref, row_ref, out_ref):
     bins, width = row_ref.shape
-    for channel in range(out_ref.shape[0] // bins):
+    block = out_ref.shape[0]
+    odd = odd_ref[0] > 0
+    for channel in range(block // bins):
+        rows = slice(channel * bins, (channel + 1) * bins)
         shifted = pltpu.roll(row_ref[...], channel * bins, axis=1)
-        out_ref[channel * bins : (channel + 1) * bins, :] = shifted.astype(jnp.bfloat16)
-
-
-def banded(smooth_kernel, channels_here, bins):
+        low, high = shifted[:, :block], shifted[:, width - block :]
+        out_ref[rows, :block] = jnp.where(odd, low, high).astype(jnp.bfloat16)
+        out_ref[rows, block : width - block] = shifted[:, block : width - block].astype(jnp.bfloat16)
+        out_ref[rows, width - block :] = jnp.where(odd, high, low).astype(jnp.bfloat16)
+
+
+def banded(smooth_kernel, odd, channels_here, bins):
     extent = smooth_kernel.shape[0]
     half = extent // 2
     stored = np.arange(bins) // 8 + np.arange(bins) % 8 * (bins // 8)
@@ -224,17 +250,17 @@
     return pl.pallas_call(
         band_kernel,
         out_shape=jax.ShapeDtypeStruct((channels_here * bins, width), jnp.bfloat16),
-        in_specs=[vmem],
+        in_specs=[pl.BlockSpec(memory_space=pltpu.SMEM), vmem],
         out_specs=vmem,
         compiler_params=pltpu.CompilerParams(vmem_limit_bytes=16 << 20),
         name="band",
-    )(row)
-
-
-def smooth_body(low_ref, mid_ref, high_ref, matrix_ref, out_ref):
+    )(odd.astype(jnp.int32).reshape(1), row)
+
+
+def smooth_body(pair_ref, mid_ref, next_ref, matrix_ref, out_ref):
     channels, bins, beams = mid_ref.shape
     centered = []
-    for ref in (low_ref, mid_ref, high_ref):
+    for ref in (pair_ref, mid_ref, next_ref):
         values = ref[...].astype(jnp.float32)
         values = values - jnp.mean(values, axis=1, keepdims=True)
         centered.append(values.astype(jnp.bfloat16).reshape(channels * bins, beams))
@@ -243,7 +269,7 @@
     out_ref[...] = result.reshape(channels, bins, beams)
 
 
-def smooth(low, mid, high, matrix):
+def smooth(pair, mid, other, matrix):
     vmem = pl.BlockSpec(memory_space=pltpu.VMEM)
     return pl.pallas_call(
         smooth_body,
@@ -252,7 +278,7 @@
         out_specs=vmem,
         compiler_params=pltpu.CompilerParams(vmem_limit_bytes=16 << 20),
         name="smooth",
-    )(low, mid, high, matrix)
+    )(pair, mid, other, matrix)
 
 
 def body(samples, filter_taps, beam_weights, smooth_kernel):
@@ -262,17 +288,18 @@
     voltage, smooth_kernel = lax.optimization_barrier((voltage, smooth_kernel))
     turned = lax.all_to_all(voltage, ("wide", "narrow"), split_axis=0, concat_axis=0, tiled=True)
     per_device, spectra = turned.shape[1], turned.shape[4]
-    matrix = banded(smooth_kernel, per_device * wide_count, spectra // INTEG)
+    odd = lax.axis_index("narrow") % 2
+    matrix = banded(smooth_kernel, odd, per_device * wide_count, spectra // INTEG)
     turned, matrix = lax.optimization_barrier((turned, matrix))
     intensity = beam_power(turned, beam_weights, wide_count)
     bins, beams = intensity.shape[2], intensity.shape[3]
     by_beam = lax.all_to_all(intensity, "wide", split_axis=0, concat_axis=0, tiled=True)
     by_beam = by_beam.reshape(-1, bins, beams)
-    forward = [(i, i + 1) for i in range(narrow_count - 1)]
-    backward = [(target, source) for source, target in forward]
-    low = lax.ppermute(by_beam, "narrow", forward)
-    high = lax.ppermute(by_beam, "narrow", backward)
-    return smooth(low, by_beam, high, matrix)
+    pairs = [(i, i ^ 1) for i in range(narrow_count)]
+    others = [(i, i - 1 + i % 2 * 2) for i in range(1, narrow_count - 1)]
+    other = lax.ppermute(by_beam, "narrow", others)
+    pair = lax.ppermute(by_beam, "narrow", pairs)
+    return smooth(pair, by_beam, other, matrix)
 
 
 def solution(mesh):

time: 98.9 us -> 100 us (1.011)
  Pallas kernels: 26.5 us -> 28.4 us
  starting transfers between devices: 16.3 us -> 14.9 us
    pallas_call x1, Pallas kernels: 13 us -> 14.8 us  [channelize(): pl.pallas_call(functools.partial(channelize_kernel, frames, spectra, tap_...]
    ppermute x2, starting transfers between devices: 5.41 us -> 4.08 us  [the longest x1 3.49 us: body(): other = lax.ppermute(by_beam, 'narrow', others)]
  transfers between devices with their start and end apart: 3 -> 3, of which waited for: 3 -> 2; matrix products, arithmetic and copies ran while one was open for 1% -> 1% of each run, Pallas kernels for 1% -> 1%
where the time goes in v2:
time: 100 us; the launch traced here: 98.9 us
  waiting for transfers between devices  45.3 us (45%)
  Pallas kernels  28.4 us (28%)
  starting transfers between devices  14.9 us (15%)
  blocking collectives  9.57 us (10%)
    all_to_all x1, waiting for transfers between devices, body(): lax.all_to_all(voltage, ('wide', 'narrow'), split_axis=0, concat_axis=0,...  38 us
    pallas_call x1, Pallas kernels, channelize(): pl.pallas_call(functools.partial(channelize_kernel, frames, spectra, tap_...  14.8 us
    all_to_all x1, starting transfers between devices, body(): lax.all_to_all(voltage, ('wide', 'narrow'), split_axis=0, concat_axis=0,...  10.9 us
    pallas_call x1, Pallas kernels, beam_power(): pl.pallas_call(functools.partial(beam_kernel, 1.0 / (pols * INTEG)), out_...  10.7 us
    all_to_all x1, blocking collectives, body(): lax.all_to_all(intensity, 'wide', split_axis=0, concat_axis=0, tiled=True)  9.57 us
    ppermute x1, waiting for transfers between devices, body(): other = lax.ppermute(by_beam, 'narrow', others)  7.33 us
    ppermute x1, starting transfers between devices, body(): other = lax.ppermute(by_beam, 'narrow', others)  3.49 us
  transfers between devices with their start and end apart: 3, of which 2 were waited for; matrix products, arithmetic and copies ran while one was open for 1% of the time, Pallas kernels for 1%

profile of v2, /device:TPU:8, one launch (start us, length us, event | category | flops | bytes accessed | tf_op | source)
XLA Modules:
  0.0 98.9 jit_solution(7389060086077533357)
XLA Ops:
  0.0 14.8 %channelize.1 = bf16[128,2,16,384]{3,2,1,0:T(8,128)(2,1)} custom-call(bf16[12768,128]{1,0:T(8,128)(2,1)} %bitcast.18, f32[16,256]{1,0:T(8,128)} %taps_ref.1, bf16[2,256,768]{2,1,0:T(8,128)(2,1)} %constant.24.clone.table_ref), custom_call_target="tpu_custom_call" | custom-call | tf_op jit(solution)/shard_map/channelize/pallas_call | solution.py:148
  14.8 0.0 copy-start
  14.8 0.0 copy-start.1
  14.8 10.9 %all-to-all-start = ((bf16[128,2,2,8,384]{4,3,2,1,0:T(8,128)(2,1)}), bf16[128,2,2,8,384]{4,3,2,1,0:T(8,128)(2,1)}, u32[]{:S(2)}, u32[]{:S(2)}) async-start(bf16[128,2,2,8,384]{4,3,2,1,0:T(8,128)(2,1)} %bitcast.17), calls=%async_computation | async-start | bytes 6291456 | tf_op jit(solution)/shard_map/all_to_all | solution.py:289
  25.7 0.0 copy-done
  25.7 0.0 copy-done.1
  25.7 0.3 convolution_bitcast_fusion
  26.0 0.3 reshape.22
  26.3 1.1 %band.1.matrix_ref = bf16[768,2304]{1,0:T(8,128)(2,1)S(1)} custom-call(s32[1]{0:T(128)} %bitcast.4.odd_ref, f32[48,2304]{1,0:T(8,128)S(1)} %pad.4.row_ref), custom_call_target="tpu_custom_call" | custom-call | tf_op jit(solution)/shard_map/band/pallas_call | solution.py:250
  27.3 38.0 %all-to-all-done.volt_ref = bf16[128,2,2,8,384]{4,3,2,1,0:T(8,128)(2,1)} async-done(((bf16[128,2,2,8,384]{4,3,2,1,0:T(8,128)(2,1)}), bf16[128,2,2,8,384]{4,3,2,1,0:T(8,128)(2,1)}, u32[]{:S(2)}, u32[]{:S(2)}) %all-to-all-start) | async-done | bytes 3145760 | tf_op jit(solution)/shard_map/all_to_all | solution.py:289
  65.3 10.7 %beam_power.1 = bf16[8,2,48,128]{3,2,1,0:T(8,128)(2,1)S(1)} custom-call(bf16[128,2,2,8,384]{4,3,2,1,0:T(8,128)(2,1)} %all-to-all-done.volt_ref, bf16[2,2,2,512,1024]{4,3,2,1,0:T(8,128)(2,1)} %weight_ref.1), custom_call_target="tpu_custom_call" | custom-call | tf_op jit(solution)/shard_map/beam_power/pallas_call | solution.py:208
  76.1 9.6 %all_to_all.10 = bf16[8,2,48,128]{3,2,1,0:T(8,128)(2,1)S(1)} all-to-all(bf16[8,2,48,128]{3,2,1,0:T(8,128)(2,1)S(1)} %beam_power.1), channel_id=1, replica_groups=mesh['wide'=8,'narrow'=16] {'wide'}, dimensions={0} | all-to-all | bytes 393216 | tf_op jit(solution)/shard_map/all_to_all | solution.py:296
  85.6 3.5 %collective-permute-start.1 = (bf16[16,48,128]{2,1,0:T(8,128)(2,1)S(1)}, bf16[16,48,128]{2,1,0:T(8,128)(2,1)S(1)}, u32[]{:S(2)}, u32[]{:S(2)}) collective-permute-start(bf16[16,48,128]{2,1,0:T(8,128)(2,1)S(1)} %bitcast.14), channel_id=1, source_target_pairs={{1,2},{2,1},{3,4},{4,3},{5,6},{6,5},{7,8},{8,7},{9,10},{10,9},{11,... | collective-permute-start | bytes 589832 | tf_op jit(solution)/shard_map/ppermute | solution.py:300
  89.2 0.6 collective-permute-start
  89.7 7.3 %collective-permute-done.1.next_ref = bf16[16,48,128]{2,1,0:T(8,128)(2,1)S(1)} collective-permute-done((bf16[16,48,128]{2,1,0:T(8,128)(2,1)S(1)}, bf16[16,48,128]{2,1,0:T(8,128)(2,1)S(1)}, u32[]{:S(2)}, u32[]{:S(2)}) %collective-permute-start.1) | collective-permute-done | bytes 196640 | tf_op jit(solution)/shard_map/ppermute | solution.py:300
  97.1 0.0 collective-permute-done.pair_ref
  97.1 1.8 %smooth.1 = f32[16,48,128]{2,1,0:T(8,128)} custom-call(bf16[16,48,128]{2,1,0:T(8,128)(2,1)S(1)} %collective-permute-done.pair_ref, bf16[16,48,128]{2,1,0:T(8,128)(2,1)S(1)} %bitcast.16, bf16[16,48,128]{2,1,0:T(8,128)(2,1)S(1)} %collective-permute-done.1.next_ref, bf16[768,2304]{1,0:T(8,128)(2,1)S(1)} %band.1.matrix_ref), custom_call_target="tpu_custom_call" | custom-call | tf_op jit(solution)/shard_map/smooth/pallas_call | solution.py:274
  (1 shorter events, 0.0 us)
Async XLA Ops:
  14.8 10.9 %copy-start = (bf16[33,48,48]{2,0,1:T(8,128)(2,1)S(1)}, bf16[33,48,48]{2,0,1:T(8,128)(2,1)}, u32[]{:S(2)}) copy-start(bf16[33,48,48]{2,0,1:T(8,128)(2,1)} %constant.25.clone) | copy-start | bytes 456196
  14.8 10.9 %copy-start.1 = (f32[33,33]{1,0:T(8,128)S(1)}, f32[33,33]{1,0:T(8,128)}, u32[]{:S(2)}) copy-start(f32[33,33]{1,0:T(8,128)} %param.9) | copy-start | bytes 13072
  14.8 50.6 %all-to-all-start = ((bf16[128,2,2,8,384]{4,3,2,1,0:T(8,128)(2,1)}), bf16[128,2,2,8,384]{4,3,2,1,0:T(8,128)(2,1)}, u32[]{:S(2)}, u32[]{:S(2)}) async-start(bf16[128,2,2,8,384]{4,3,2,1,0:T(8,128)(2,1)} %bitcast.17), calls=%async_computation | async-start | bytes 6291456 | tf_op jit(solution)/shard_map/all_to_all | solution.py:289
  85.6 11.4 %collective-permute-start.1 = (bf16[16,48,128]{2,1,0:T(8,128)(2,1)S(1)}, bf16[16,48,128]{2,1,0:T(8,128)(2,1)S(1)}, u32[]{:S(2)}, u32[]{:S(2)}) collective-permute-start(bf16[16,48,128]{2,1,0:T(8,128)(2,1)S(1)} %bitcast.14), channel_id=1, source_target_pairs={{1,2},{2,1},{3,4},{4,3},{5,6},{6,5},{7,8},{8,7},{9,10},{10,9},{11,... | collective-permute-start | bytes 589832 | tf_op jit(solution)/shard_map/ppermute | solution.py:300
  89.2 7.9 %collective-permute-start = (bf16[16,48,128]{2,1,0:T(8,128)(2,1)S(1)}, bf16[16,48,128]{2,1,0:T(8,128)(2,1)S(1)}, u32[]{:S(2)}, u32[]{:S(2)}) collective-permute-start(bf16[16,48,128]{2,1,0:T(8,128)(2,1)S(1)} %bitcast.15), channel_id=1, source_target_pairs={{0,1},{1,0},{2,3},{3,2},{4,5},{5,4},{6,7},{7,6},{8,9},{9,8},{10,11... | collective-permute-start | bytes 589832 | tf_op jit(solution)/shard_map/ppermute | solution.py:301

commit v3 on v2

--- a/solution.py
+++ b/solution.py
@@ -15,10 +15,9 @@
 BATCH = 2
 
 
-def fourier_table(points, wide_count, narrow_count):
-    per_device = points // (wide_count * narrow_count)
-    slot = np.arange(wide_count * narrow_count)
-    first = (slot % narrow_count * wide_count + slot // narrow_count) * per_device
+def fourier_table(points, owners):
+    per_device = points // owners
+    first = np.arange(owners) * per_device
     channel = first[None, :] + np.arange(per_device)[:, None]
     angle = (channel[:, :, None] * np.arange(points // 2) % points) * (2.0 * np.pi / points)
     cosine = np.cos(angle) / np.sqrt(points)
@@ -33,7 +32,7 @@
 
 
 def channelize_kernel(
-    frames, spectra, tap_count, group, x_ref, taps_ref, table_ref, out_ref, lined, windowed, turned
+    frames, spectra, tap_count, group, x_ref, taps_ref, table_ref, out_ref, lined, windowed, turned, packed, sent
 ):
     step = pl.program_id(0)
     rows = x_ref.shape[0] // group
@@ -122,26 +121,35 @@
 
     @pl.when(step == pl.num_programs(0) - 1)
     def _():
-        for column in range(spectra // LANES):
-            columns = slice(column * LANES, (column + 1) * LANES)
-            for parity in range(parities):
-                count = outputs * inputs_here
-                values = turned[column, parity * count : (parity + 1) * count, :].astype(jnp.bfloat16)
-                out_ref[:, parity, :, columns] = values.reshape(out_ref.shape[0], -1, LANES)
-
-
-def channelize(samples, filter_taps, wide_count, narrow_count):
+        chunks = sent.shape[0]
+        owners = packed.shape[0] // chunks
+        count = outputs * inputs_here // chunks
+        copies = []
+        for chunk in range(chunks):
+            here = slice(chunk * owners, (chunk + 1) * owners)
+            for column in range(spectra // LANES):
+                columns = slice(column * LANES, (column + 1) * LANES)
+                for parity in range(parities):
+                    start = (parity * chunks + chunk) * count
+                    values = turned[column, start : start + count, :].astype(jnp.bfloat16)
+                    packed[here, parity, :, columns] = values.reshape(owners, -1, LANES)
+            copies.append(pltpu.make_async_copy(packed.at[here], out_ref.at[here], sent.at[chunk]))
+            copies[-1].start()
+        for copy in copies:
+            copy.wait()
+
+
+def channelize(samples, filter_taps, owners):
     inputs_here, _, length = samples.shape
     tap_count, points = filter_taps.shape
     frames = length // points
     spectra = frames - tap_count + 1
     halves = points // LANES
     group = 4
-    table = fourier_table(points, wide_count, narrow_count)
+    table = fourier_table(points, owners)
     lined = samples.reshape(inputs_here, 2, frames, halves, LANES).transpose(0, 2, 3, 1, 4)
     lined = lined.reshape(-1, LANES)
     rows = lined.shape[0] // inputs_here * group
-    owners = wide_count * narrow_count
     shape = (owners, points // owners, 2 * inputs_here, spectra)
     pitch = -(-(spectra // 8 + tap_count - 1) * 2 * halves // 8) * 64
     whole = lambda array: pl.BlockSpec(array.shape, lambda i: (0,) * array.ndim)
@@ -154,11 +162,13 @@
             whole(filter_taps),
             whole(table),
         ],
-        out_specs=pl.BlockSpec(shape, lambda i: (0, 0, 0, 0)),
+        out_specs=pl.BlockSpec(memory_space=pl.ANY),
         scratch_shapes=[
             pltpu.VMEM((group * pitch, LANES), jnp.float32),
             pltpu.VMEM((group * spectra, 2 * points), jnp.float32),
             pltpu.VMEM((spectra // LANES, 2 * points * inputs_here, LANES), jnp.float32),
+            pltpu.VMEM(shape, jnp.bfloat16),
+            pltpu.SemaphoreType.DMA((4,)),
         ],
         compiler_params=pltpu.CompilerParams(vmem_limit_bytes=60 << 20),
         name="channelize",
@@ -167,11 +177,19 @@
 
 
 def beam_kernel(scale, volt_ref, weight_ref, out_ref, held, arrived):
-    sources, per_device, _, inputs, spectra = volt_ref.shape
+    inner, outer, per_device, _, inputs, spectra = volt_ref.shape
     pols, beams = weight_ref.shape[1], weight_ref.shape[-1]
-    each = sources // pols
-    dishes = each * inputs
+    each = outer // pols
+    dishes = each * inner * inputs
     owners, chunk = out_ref.shape[0], out_ref.shape[-1]
+
+    def gathered(channel, pol, part):
+        blocks = [
+            volt_ref[:, source, channel, part].reshape(inner * inputs, spectra)
+            for source in range(pol * each, (pol + 1) * each)
+        ]
+        return jnp.concatenate(blocks, axis=0).T
+
     copies = {}
     for channel in range(per_device):
         for pol in range(pols):
@@ -182,9 +200,8 @@
     for channel in range(per_device):
         total = None
         for pol in range(pols):
-            rows = slice(pol * each, (pol + 1) * each)
-            real = volt_ref[rows, channel, 0].reshape(dishes, spectra).T
-            imag = volt_ref[rows, channel, 1].reshape(dishes, spectra).T
+            real = gathered(channel, pol, 0)
+            imag = gathered(channel, pol, 1)
             lhs = jnp.concatenate(
                 [jnp.concatenate([real, -imag], axis=1), jnp.concatenate([imag, real], axis=1)], axis=0
             )
@@ -201,7 +218,7 @@
 
 
 def beam_power(turned, weights, wide_count):
-    per_device, spectra = turned.shape[1], turned.shape[4]
+    per_device, spectra = turned.shape[2], turned.shape[5]
     pols, beams = weights.shape[1], weights.shape[4]
     bins = spectra // INTEG
     vmem = pl.BlockSpec(memory_space=pltpu.VMEM)
@@ -257,37 +274,57 @@
     )(odd.astype(jnp.int32).reshape(1), row)
 
 
-def smooth_body(pair_ref, mid_ref, next_ref, matrix_ref, out_ref):
-    channels, bins, beams = mid_ref.shape
+def filtered(refs, matrix):
     centered = []
-    for ref in (pair_ref, mid_ref, next_ref):
+    for ref in refs:
+        channels, bins, beams = ref.shape
         values = ref[...].astype(jnp.float32)
         values = values - jnp.mean(values, axis=1, keepdims=True)
         centered.append(values.astype(jnp.bfloat16).reshape(channels * bins, beams))
     stacked = jnp.concatenate(centered, axis=0)
-    result = jnp.dot(matrix_ref[...], stacked, preferred_element_type=jnp.float32)
-    out_ref[...] = result.reshape(channels, bins, beams)
+    return jnp.dot(matrix, stacked, preferred_element_type=jnp.float32)
+
+
+def near_kernel(pair_ref, mid_ref, matrix_ref, out_ref):
+    width = out_ref.shape[0]
+    out_ref[...] = filtered((pair_ref, mid_ref), matrix_ref[:, : 2 * width])
+
+
+def far_kernel(other_ref, part_ref, matrix_ref, out_ref):
+    width = part_ref.shape[0]
+    result = part_ref[...] + filtered((other_ref,), matrix_ref[:, 2 * width :])
+    out_ref[...] = result.reshape(out_ref.shape)
 
 
 def smooth(pair, mid, other, matrix):
+    channels, bins, beams = mid.shape
     vmem = pl.BlockSpec(memory_space=pltpu.VMEM)
-    return pl.pallas_call(
-        smooth_body,
-        out_shape=jax.ShapeDtypeStruct(mid.shape, jnp.float32),
-        in_specs=[vmem] * 4,
+    near = pl.pallas_call(
+        near_kernel,
+        out_shape=jax.ShapeDtypeStruct((channels * bins, beams), jnp.float32),
+        in_specs=[vmem] * 3,
         out_specs=vmem,
         compiler_params=pltpu.CompilerParams(vmem_limit_bytes=16 << 20),
-        name="smooth",
-    )(pair, mid, other, matrix)
+        name="smooth_near",
+    )(pair, mid, matrix)
+    return pl.pallas_call(
+        far_kernel,
+        out_shape=jax.ShapeDtypeStruct(mid.shape, jnp.float32),
+        in_specs=[vmem] * 3,
+        out_specs=vmem,
+        compiler_params=pltpu.CompilerParams(vmem_limit_bytes=16 << 20),
+        name="smooth_far",
+    )(other, near, matrix)
 
 
 def body(samples, filter_taps, beam_weights, smooth_kernel):
     wide_count = lax.axis_size("wide")
     narrow_count = lax.axis_size("narrow")
-    voltage = channelize(samples, filter_taps, wide_count, narrow_count)
+    voltage = channelize(samples, filter_taps, wide_count * narrow_count)
     voltage, smooth_kernel = lax.optimization_barrier((voltage, smooth_kernel))
-    turned = lax.all_to_all(voltage, ("wide", "narrow"), split_axis=0, concat_axis=0, tiled=True)
-    per_device, spectra = turned.shape[1], turned.shape[4]
+    turned = lax.all_to_all(voltage, ("narrow", "wide"), split_axis=0, concat_axis=0, tiled=True)
+    turned = turned.reshape(narrow_count, wide_count, *turned.shape[1:])
+    per_device, spectra = turned.shape[2], turned.shape[5]
     odd = lax.axis_index("narrow") % 2
     matrix = banded(smooth_kernel, odd, per_device * wide_count, spectra // INTEG)
     turned, matrix = lax.optimization_barrier((turned, matrix))

time: 100 us -> 101 us (1.010); the launches traced: 98.9 us -> 98.9 us
    all_to_all x1, waiting for transfers between devices: 38 us -> 39.5 us  [body(): lax.all_to_all(voltage, ('narrow', 'wide'), split_axis=0, concat_axis=0,...]
    ppermute x1, waiting for transfers between devices: 7.33 us -> 5.92 us  [body(): other = lax.ppermute(by_beam, 'narrow', others)]
    pallas_call x1 -> x2, Pallas kernels: 1.85 us -> 2.03 us  [the longest x1 1.24 us: smooth(): pl.pallas_call(far_kernel, out_shape=jax.ShapeDtypeStruct(mid.shape, jnp....]
  transfers between devices with their start and end apart: 3 -> 3, of which waited for: 2 -> 2; matrix products, arithmetic and copies ran while one was open for 1% -> 1% of each run, Pallas kernels for 1% -> 2%
where the time goes in v3:
time: 101 us; the launch traced here: 98.9 us
  waiting for transfers between devices  45.4 us (45%)
  Pallas kernels  28.3 us (28%)
  starting transfers between devices  15.1 us (15%)
  blocking collectives  9.36 us (9%)
    all_to_all x1, waiting for transfers between devices, body(): lax.all_to_all(voltage, ('narrow', 'wide'), split_axis=0, concat_axis=0,...  39.5 us
    pallas_call x1, Pallas kernels, channelize(): pl.pallas_call(functools.partial(channelize_kernel, frames, spectra, tap_...  14.5 us
    all_to_all x1, starting transfers between devices, body(): lax.all_to_all(voltage, ('narrow', 'wide'), split_axis=0, concat_axis=0,...  10.9 us
    pallas_call x1, Pallas kernels, beam_power(): pl.pallas_call(functools.partial(beam_kernel, 1.0 / (pols * INTEG)), out_...  10.7 us
    all_to_all x1, blocking collectives, body(): lax.all_to_all(intensity, 'wide', split_axis=0, concat_axis=0, tiled=True)  9.36 us
    ppermute x1, waiting for transfers between devices, body(): other = lax.ppermute(by_beam, 'narrow', others)  5.92 us
    ppermute x1, starting transfers between devices, body(): other = lax.ppermute(by_beam, 'narrow', others)  4.2 us
  transfers between devices with their start and end apart: 3, of which 2 were waited for; matrix products, arithmetic and copies ran while one was open for 1% of the time, Pallas kernels for 2%

profile of v3, /device:TPU:8, one launch (start us, length us, event | category | flops | bytes accessed | tf_op | source)
XLA Modules:
  0.0 98.9 jit_solution(6349164693065714156)
XLA Ops:
  0.0 14.5 %channelize.1 = bf16[128,2,16,384]{3,2,1,0:T(8,128)(2,1)} custom-call(bf16[12768,128]{1,0:T(8,128)(2,1)} %bitcast.19, f32[16,256]{1,0:T(8,128)} %taps_ref.1, bf16[2,256,768]{2,1,0:T(8,128)(2,1)} %constant.24.clone.table_ref), custom_call_target="tpu_custom_call" | custom-call | tf_op jit(solution)/shard_map/channelize/pallas_call | solution.py:156
  14.5 0.0 copy-start
  14.5 0.0 copy-start.1
  14.5 10.9 %all-to-all-start = ((bf16[128,2,2,8,384]{4,3,2,1,0:T(8,128)(2,1)}), bf16[128,2,2,8,384]{4,3,2,1,0:T(8,128)(2,1)}, u32[]{:S(2)}, u32[]{:S(2)}) async-start(bf16[128,2,2,8,384]{4,3,2,1,0:T(8,128)(2,1)} %bitcast.18), calls=%async_computation | async-start | bytes 6291456 | tf_op jit(solution)/shard_map/all_to_all | solution.py:325
  25.4 0.0 copy-done
  25.4 0.0 copy-done.1
  25.4 0.3 convolution_bitcast_fusion
  25.7 0.3 reshape.26
  26.0 1.1 %band.1.matrix_ref = bf16[768,2304]{1,0:T(8,128)(2,1)S(1)} custom-call(s32[1]{0:T(128)} %bitcast.5.odd_ref, f32[48,2304]{1,0:T(8,128)S(1)} %pad.4.row_ref), custom_call_target="tpu_custom_call" | custom-call | tf_op jit(solution)/shard_map/band/pallas_call | solution.py:267
  27.1 39.5 %all-to-all-done = bf16[128,2,2,8,384]{4,3,2,1,0:T(8,128)(2,1)} async-done(((bf16[128,2,2,8,384]{4,3,2,1,0:T(8,128)(2,1)}), bf16[128,2,2,8,384]{4,3,2,1,0:T(8,128)(2,1)}, u32[]{:S(2)}, u32[]{:S(2)}) %all-to-all-start) | async-done | bytes 3145760 | tf_op jit(solution)/shard_map/all_to_all | solution.py:325
  66.6 10.7 %beam_power.1 = bf16[8,2,48,128]{3,2,1,0:T(8,128)(2,1)S(1)} custom-call(bf16[16,8,2,2,8,384]{5,4,3,2,1,0:T(8,128)(2,1)} %bitcast.4.volt_ref, bf16[2,2,2,512,1024]{4,3,2,1,0:T(8,128)(2,1)} %weight_ref.1), custom_call_target="tpu_custom_call" | custom-call | tf_op jit(solution)/shard_map/beam_power/pallas_call | solution.py:225
  77.3 9.4 %all_to_all.10 = bf16[8,2,48,128]{3,2,1,0:T(8,128)(2,1)S(1)} all-to-all(bf16[8,2,48,128]{3,2,1,0:T(8,128)(2,1)S(1)} %beam_power.1), channel_id=1, replica_groups=mesh['wide'=8,'narrow'=16] {'wide'}, dimensions={0} | all-to-all | bytes 393216 | tf_op jit(solution)/shard_map/all_to_all | solution.py:333
  86.7 0.0 collective-permute-start.1
  86.7 4.2 %collective-permute-start = (bf16[16,48,128]{2,1,0:T(8,128)(2,1)S(1)}, bf16[16,48,128]{2,1,0:T(8,128)(2,1)S(1)}, u32[]{:S(2)}, u32[]{:S(2)}) collective-permute-start(bf16[16,48,128]{2,1,0:T(8,128)(2,1)S(1)} %bitcast.16), channel_id=1, source_target_pairs={{1,2},{2,1},{3,4},{4,3},{5,6},{6,5},{7,8},{8,7},{9,10},{10,9},{11,... | collective-permute-start | bytes 589832 | tf_op jit(solution)/shard_map/ppermute | solution.py:337
  90.9 0.0 collective-permute-done.1.pair_ref
  90.9 0.8 smooth_near.1.part_ref
  91.7 5.9 %collective-permute-done.other_ref = bf16[16,48,128]{2,1,0:T(8,128)(2,1)S(1)} collective-permute-done((bf16[16,48,128]{2,1,0:T(8,128)(2,1)S(1)}, bf16[16,48,128]{2,1,0:T(8,128)(2,1)S(1)}, u32[]{:S(2)}, u32[]{:S(2)}) %collective-permute-start) | collective-permute-done | bytes 196640 | tf_op jit(solution)/shard_map/ppermute | solution.py:337
  97.6 1.2 %smooth_far.1 = f32[16,48,128]{2,1,0:T(8,128)} custom-call(bf16[16,48,128]{2,1,0:T(8,128)(2,1)S(1)} %collective-permute-done.other_ref, f32[768,128]{1,0:T(8,128)S(1)} %smooth_near.1.part_ref, bf16[768,2304]{1,0:T(8,128)(2,1)S(1)} %band.1.matrix_ref), custom_call_target="tpu_custom_call" | custom-call | tf_op jit(solution)/shard_map/smooth_far/pallas_call | solution.py:310
  (1 shorter events, 0.0 us)
Async XLA Ops:
  14.5 10.9 %copy-start = (bf16[33,48,48]{2,0,1:T(8,128)(2,1)S(1)}, bf16[33,48,48]{2,0,1:T(8,128)(2,1)}, u32[]{:S(2)}) copy-start(bf16[33,48,48]{2,0,1:T(8,128)(2,1)} %constant.25.clone) | copy-start | bytes 456196
  14.5 10.9 %copy-start.1 = (f32[33,33]{1,0:T(8,128)S(1)}, f32[33,33]{1,0:T(8,128)}, u32[]{:S(2)}) copy-start(f32[33,33]{1,0:T(8,128)} %param.9) | copy-start | bytes 13072
  14.5 52.1 %all-to-all-start = ((bf16[128,2,2,8,384]{4,3,2,1,0:T(8,128)(2,1)}), bf16[128,2,2,8,384]{4,3,2,1,0:T(8,128)(2,1)}, u32[]{:S(2)}, u32[]{:S(2)}) async-start(bf16[128,2,2,8,384]{4,3,2,1,0:T(8,128)(2,1)} %bitcast.18), calls=%async_computation | async-start | bytes 6291456 | tf_op jit(solution)/shard_map/all_to_all | solution.py:325
  86.7 4.2 %collective-permute-start.1 = (bf16[16,48,128]{2,1,0:T(8,128)(2,1)S(1)}, bf16[16,48,128]{2,1,0:T(8,128)(2,1)S(1)}, u32[]{:S(2)}, u32[]{:S(2)}) collective-permute-start(bf16[16,48,128]{2,1,0:T(8,128)(2,1)S(1)} %bitcast.15), channel_id=1, source_target_pairs={{0,1},{1,0},{2,3},{3,2},{4,5},{5,4},{6,7},{7,6},{8,9},{9,8},{10,11... | collective-permute-start | bytes 589832 | tf_op jit(solution)/shard_map/ppermute | solution.py:338
  86.7 10.9 %collective-permute-start = (bf16[16,48,128]{2,1,0:T(8,128)(2,1)S(1)}, bf16[16,48,128]{2,1,0:T(8,128)(2,1)S(1)}, u32[]{:S(2)}, u32[]{:S(2)}) collective-permute-start(bf16[16,48,128]{2,1,0:T(8,128)(2,1)S(1)} %bitcast.16), channel_id=1, source_target_pairs={{1,2},{2,1},{3,4},{4,3},{5,6},{6,5},{7,8},{8,7},{9,10},{10,9},{11,... | collective-permute-start | bytes 589832 | tf_op jit(solution)/shard_map/ppermute | solution.py:337

commit v4 on v3

--- a/solution.py
+++ b/solution.py
@@ -214,7 +214,9 @@
             total = power if total is None else total + power
         total = (total.reshape(spectra // INTEG, beams) * jnp.float32(scale)).astype(jnp.bfloat16)
         for owner in range(owners):
-            out_ref[owner, channel] = total[:, owner * chunk : (owner + 1) * chunk]
+            values = total[:, owner * chunk : (owner + 1) * chunk]
+            out_ref[owner, 0, channel] = values
+            out_ref[owner ^ 1, 1, channel] = values
 
 
 def beam_power(turned, weights, wide_count):
@@ -224,7 +226,7 @@
     vmem = pl.BlockSpec(memory_space=pltpu.VMEM)
     return pl.pallas_call(
         functools.partial(beam_kernel, 1.0 / (pols * INTEG)),
-        out_shape=jax.ShapeDtypeStruct((wide_count, per_device, bins, beams // wide_count), jnp.bfloat16),
+        out_shape=jax.ShapeDtypeStruct((wide_count, 2, per_device, bins, beams // wide_count), jnp.bfloat16),
         in_specs=[vmem, pl.BlockSpec(memory_space=pl.ANY)],
         out_specs=vmem,
         scratch_shapes=[
@@ -329,14 +331,19 @@
     matrix = banded(smooth_kernel, odd, per_device * wide_count, spectra // INTEG)
     turned, matrix = lax.optimization_barrier((turned, matrix))
     intensity = beam_power(turned, beam_weights, wide_count)
-    bins, beams = intensity.shape[2], intensity.shape[3]
+    bins, beams = intensity.shape[3], intensity.shape[4]
     by_beam = lax.all_to_all(intensity, "wide", split_axis=0, concat_axis=0, tiled=True)
-    by_beam = by_beam.reshape(-1, bins, beams)
+    own = by_beam[:, 0].reshape(-1, bins, beams)
+    lent = by_beam[:, 1].reshape(-1, bins, beams)
     pairs = [(i, i ^ 1) for i in range(narrow_count)]
-    others = [(i, i - 1 + i % 2 * 2) for i in range(1, narrow_count - 1)]
-    other = lax.ppermute(by_beam, "narrow", others)
-    pair = lax.ppermute(by_beam, "narrow", pairs)
-    return smooth(pair, by_beam, other, matrix)
+    others = [
+        (w * narrow_count + i, (w ^ 1) * narrow_count + i - 1 + i % 2 * 2)
+        for i in range(1, narrow_count - 1)
+        for w in range(wide_count)
+    ]
+    other = lax.ppermute(lent, ("wide", "narrow"), others)
+    pair = lax.ppermute(own, "narrow", pairs)
+    return smooth(pair, own, other, matrix)
 
 
 def solution(mesh):

time: 101 us -> 102 us (level)
  blocking collectives: 9.36 us -> 10.5 us
    all_to_all x1, blocking collectives: 9.36 us -> 10.5 us  [body(): lax.all_to_all(intensity, 'wide', split_axis=0, concat_axis=0, tiled=True)]
where the time goes in v4:
time: 102 us; the launch traced here: 99.6 us
  waiting for transfers between devices  45.7 us (45%)
  Pallas kernels  28.3 us (28%)
  starting transfers between devices  14.4 us (14%)
  blocking collectives  10.5 us (10%)
    all_to_all x1, waiting for transfers between devices, body(): lax.all_to_all(voltage, ('narrow', 'wide'), split_axis=0, concat_axis=0,...  39.5 us
    pallas_call x1, Pallas kernels, channelize(): pl.pallas_call(functools.partial(channelize_kernel, frames, spectra, tap_...  14.5 us
    all_to_all x1, starting transfers between devices, body(): lax.all_to_all(voltage, ('narrow', 'wide'), split_axis=0, concat_axis=0,...  10.9 us
    pallas_call x1, Pallas kernels, beam_power(): pl.pallas_call(functools.partial(beam_kernel, 1.0 / (pols * INTEG)), out_...  10.7 us
    all_to_all x1, blocking collectives, body(): lax.all_to_all(intensity, 'wide', split_axis=0, concat_axis=0, tiled=True)  10.5 us
    ppermute x1, waiting for transfers between devices, body(): other = lax.ppermute(lent, ('wide', 'narrow'), others)  6.14 us
    ppermute x1, starting transfers between devices, body(): other = lax.ppermute(lent, ('wide', 'narrow'), others)  3.45 us
  transfers between devices with their start and end apart: 3, of which 2 were waited for; matrix products, arithmetic and copies ran while one was open for 1% of the time, Pallas kernels for 2%

profile of v4, /device:TPU:8, one launch (start us, length us, event | category | flops | bytes accessed | tf_op | source)
XLA Modules:
  0.0 99.6 jit_solution(13570542414609689119)
XLA Ops:
  0.0 14.5 %channelize.1 = bf16[128,2,16,384]{3,2,1,0:T(8,128)(2,1)} custom-call(bf16[12768,128]{1,0:T(8,128)(2,1)} %bitcast.19, f32[16,256]{1,0:T(8,128)} %taps_ref.1, bf16[2,256,768]{2,1,0:T(8,128)(2,1)} %constant.24.clone.table_ref), custom_call_target="tpu_custom_call" | custom-call | tf_op jit(solution)/shard_map/channelize/pallas_call | solution.py:156
  14.5 0.0 copy-start
  14.5 0.0 copy-start.1
  14.5 10.9 %all-to-all-start = ((bf16[128,2,2,8,384]{4,3,2,1,0:T(8,128)(2,1)}), bf16[128,2,2,8,384]{4,3,2,1,0:T(8,128)(2,1)}, u32[]{:S(2)}, u32[]{:S(2)}) async-start(bf16[128,2,2,8,384]{4,3,2,1,0:T(8,128)(2,1)} %bitcast.18), calls=%async_computation | async-start | bytes 6291456 | tf_op jit(solution)/shard_map/all_to_all | solution.py:327
  25.4 0.0 copy-done
  25.4 0.0 copy-done.1
  25.4 0.3 convolution_bitcast_fusion
  25.7 0.3 reshape.23
  26.0 1.1 %band.1.matrix_ref = bf16[768,2304]{1,0:T(8,128)(2,1)S(1)} custom-call(s32[1]{0:T(128)} %bitcast.5.odd_ref, f32[48,2304]{1,0:T(8,128)S(1)} %pad.4.row_ref), custom_call_target="tpu_custom_call" | custom-call | tf_op jit(solution)/shard_map/band/pallas_call | solution.py:269
  27.1 39.5 %all-to-all-done = bf16[128,2,2,8,384]{4,3,2,1,0:T(8,128)(2,1)} async-done(((bf16[128,2,2,8,384]{4,3,2,1,0:T(8,128)(2,1)}), bf16[128,2,2,8,384]{4,3,2,1,0:T(8,128)(2,1)}, u32[]{:S(2)}, u32[]{:S(2)}) %all-to-all-start) | async-done | bytes 3145760 | tf_op jit(solution)/shard_map/all_to_all | solution.py:327
  66.6 10.7 %beam_power.1 = bf16[8,2,2,48,128]{4,3,2,1,0:T(8,128)(2,1)S(1)} custom-call(bf16[16,8,2,2,8,384]{5,4,3,2,1,0:T(8,128)(2,1)} %bitcast.4.volt_ref, bf16[2,2,2,512,1024]{4,3,2,1,0:T(8,128)(2,1)} %weight_ref.1), custom_call_target="tpu_custom_call" | custom-call | tf_op jit(solution)/shard_map/beam_power/pallas_call | solution.py:227
  77.3 10.5 %all_to_all.10 = bf16[8,2,2,48,128]{4,3,2,1,0:T(8,128)(2,1)S(1)} all-to-all(bf16[8,2,2,48,128]{4,3,2,1,0:T(8,128)(2,1)S(1)} %beam_power.1), channel_id=1, replica_groups=mesh['wide'=8,'narrow'=16] {'wide'}, dimensions={0} | all-to-all | bytes 786432 | tf_op jit(solution)/shard_map/all_to_all | solution.py:335
  87.9 0.1 collective-permute-start.1
  88.0 3.5 %collective-permute-start = (bf16[16,48,128]{2,1,0:T(8,128)(2,1)S(1)}, bf16[16,48,128]{2,1,0:T(8,128)(2,1)S(1)}, u32[]{:S(2)}, u32[]{:S(2)}) collective-permute-start(bf16[16,48,128]{2,1,0:T(8,128)(2,1)S(1)} %bitcast.20), channel_id=1, source_target_pairs={{1,18},{17,2},{33,50},{49,34},{65,82},{81,66},{97,114},{113,98},{2... | collective-permute-start | bytes 589832 | tf_op jit(solution)/shard_map/ppermute | solution.py:344
  91.4 0.0 collective-permute-done.1.pair_ref
  91.5 0.8 smooth_near.1.part_ref
  92.3 6.1 %collective-permute-done.other_ref = bf16[16,48,128]{2,1,0:T(8,128)(2,1)S(1)} collective-permute-done((bf16[16,48,128]{2,1,0:T(8,128)(2,1)S(1)}, bf16[16,48,128]{2,1,0:T(8,128)(2,1)S(1)}, u32[]{:S(2)}, u32[]{:S(2)}) %collective-permute-start) | collective-permute-done | bytes 196640 | tf_op jit(solution)/shard_map/ppermute | solution.py:344
  98.4 1.2 %smooth_far.1 = f32[16,48,128]{2,1,0:T(8,128)} custom-call(bf16[16,48,128]{2,1,0:T(8,128)(2,1)S(1)} %collective-permute-done.other_ref, f32[768,128]{1,0:T(8,128)S(1)} %smooth_near.1.part_ref, bf16[768,2304]{1,0:T(8,128)(2,1)S(1)} %band.1.matrix_ref), custom_call_target="tpu_custom_call" | custom-call | tf_op jit(solution)/shard_map/smooth_far/pallas_call | solution.py:312
  (2 shorter events, 0.1 us)
Async XLA Ops:
  14.5 10.9 %copy-start = (bf16[33,48,48]{2,0,1:T(8,128)(2,1)S(1)}, bf16[33,48,48]{2,0,1:T(8,128)(2,1)}, u32[]{:S(2)}) copy-start(bf16[33,48,48]{2,0,1:T(8,128)(2,1)} %constant.25.clone) | copy-start | bytes 456196
  14.5 10.9 %copy-start.1 = (f32[33,33]{1,0:T(8,128)S(1)}, f32[33,33]{1,0:T(8,128)}, u32[]{:S(2)}) copy-start(f32[33,33]{1,0:T(8,128)} %param.9) | copy-start | bytes 13072
  14.5 52.1 %all-to-all-start = ((bf16[128,2,2,8,384]{4,3,2,1,0:T(8,128)(2,1)}), bf16[128,2,2,8,384]{4,3,2,1,0:T(8,128)(2,1)}, u32[]{:S(2)}, u32[]{:S(2)}) async-start(bf16[128,2,2,8,384]{4,3,2,1,0:T(8,128)(2,1)} %bitcast.18), calls=%async_computation | async-start | bytes 6291456 | tf_op jit(solution)/shard_map/all_to_all | solution.py:327
  87.9 3.6 %collective-permute-start.1 = (bf16[16,48,128]{2,1,0:T(8,128)(2,1)S(1)}, bf16[16,48,128]{2,1,0:T(8,128)(2,1)S(1)}, u32[]{:S(2)}, u32[]{:S(2)}) collective-permute-start(bf16[16,48,128]{2,1,0:T(8,128)(2,1)S(1)} %bitcast.16), channel_id=1, source_target_pairs={{0,1},{1,0},{2,3},{3,2},{4,5},{5,4},{6,7},{7,6},{8,9},{9,8},{10,11... | collective-permute-start | bytes 589832 | tf_op jit(solution)/shard_map/ppermute | solution.py:345
  88.0 10.4 %collective-permute-start = (bf16[16,48,128]{2,1,0:T(8,128)(2,1)S(1)}, bf16[16,48,128]{2,1,0:T(8,128)(2,1)S(1)}, u32[]{:S(2)}, u32[]{:S(2)}) collective-permute-start(bf16[16,48,128]{2,1,0:T(8,128)(2,1)S(1)} %bitcast.20), channel_id=1, source_target_pairs={{1,18},{17,2},{33,50},{49,34},{65,82},{81,66},{97,114},{113,98},{2... | collective-permute-start | bytes 589832 | tf_op jit(solution)/shard_map/ppermute | solution.py:344

commit v5 on v3

--- a/solution.py
+++ b/solution.py
@@ -244,8 +244,8 @@
         rows = slice(channel * bins, (channel + 1) * bins)
         shifted = pltpu.roll(row_ref[...], channel * bins, axis=1)
         low, high = shifted[:, :block], shifted[:, width - block :]
-        out_ref[rows, :block] = jnp.where(odd, low, high).astype(jnp.bfloat16)
-        out_ref[rows, block : width - block] = shifted[:, block : width - block].astype(jnp.bfloat16)
+        out_ref[rows, :block] = shifted[:, block : width - block].astype(jnp.bfloat16)
+        out_ref[rows, block : width - block] = jnp.where(odd, low, high).astype(jnp.bfloat16)
         out_ref[rows, width - block :] = jnp.where(odd, high, low).astype(jnp.bfloat16)
 
 
@@ -285,14 +285,14 @@
     return jnp.dot(matrix, stacked, preferred_element_type=jnp.float32)
 
 
-def near_kernel(pair_ref, mid_ref, matrix_ref, out_ref):
+def near_kernel(mid_ref, matrix_ref, out_ref):
     width = out_ref.shape[0]
-    out_ref[...] = filtered((pair_ref, mid_ref), matrix_ref[:, : 2 * width])
-
-
-def far_kernel(other_ref, part_ref, matrix_ref, out_ref):
+    out_ref[...] = filtered((mid_ref,), matrix_ref[:, :width])
+
+
+def far_kernel(other_ref, pair_ref, part_ref, matrix_ref, out_ref):
     width = part_ref.shape[0]
-    result = part_ref[...] + filtered((other_ref,), matrix_ref[:, 2 * width :])
+    result = part_ref[...] + filtered((pair_ref, other_ref), matrix_ref[:, width:])
     out_ref[...] = result.reshape(out_ref.shape)
 
 
@@ -302,33 +302,32 @@
     near = pl.pallas_call(
         near_kernel,
         out_shape=jax.ShapeDtypeStruct((channels * bins, beams), jnp.float32),
-        in_specs=[vmem] * 3,
+        in_specs=[vmem] * 2,
         out_specs=vmem,
         compiler_params=pltpu.CompilerParams(vmem_limit_bytes=16 << 20),
         name="smooth_near",
-    )(pair, mid, matrix)
+    )(mid, matrix)
     return pl.pallas_call(
         far_kernel,
         out_shape=jax.ShapeDtypeStruct(mid.shape, jnp.float32),
-        in_specs=[vmem] * 3,
+        in_specs=[vmem] * 4,
         out_specs=vmem,
         compiler_params=pltpu.CompilerParams(vmem_limit_bytes=16 << 20),
         name="smooth_far",
-    )(other, near, matrix)
+    )(other, pair, near, matrix)
 
 
 def body(samples, filter_taps, beam_weights, smooth_kernel):
     wide_count = lax.axis_size("wide")
     narrow_count = lax.axis_size("narrow")
     voltage = channelize(samples, filter_taps, wide_count * narrow_count)
-    voltage, smooth_kernel = lax.optimization_barrier((voltage, smooth_kernel))
     turned = lax.all_to_all(voltage, ("narrow", "wide"), split_axis=0, concat_axis=0, tiled=True)
     turned = turned.reshape(narrow_count, wide_count, *turned.shape[1:])
     per_device, spectra = turned.shape[2], turned.shape[5]
+    intensity = beam_power(turned, beam_weights, wide_count)
+    intensity, smooth_kernel = lax.optimization_barrier((intensity, smooth_kernel))
     odd = lax.axis_index("narrow") % 2
     matrix = banded(smooth_kernel, odd, per_device * wide_count, spectra // INTEG)
-    turned, matrix = lax.optimization_barrier((turned, matrix))
-    intensity = beam_power(turned, beam_weights, wide_count)
     bins, beams = intensity.shape[2], intensity.shape[3]
     by_beam = lax.all_to_all(intensity, "wide", split_axis=0, concat_axis=0, tiled=True)
     by_beam = by_beam.reshape(-1, bins, beams)

time: 101 us -> 97.8 us (0.968); the launches traced: 98.9 us -> 97.5 us
  blocking collectives: 9.36 us -> 52 us
  waiting for transfers between devices: 45.4 us -> 11.4 us
  starting transfers between devices: 15.1 us -> 6.32 us
  Pallas kernels: 28.3 us -> 27.2 us
    all_to_all x1, blocking collectives: 9.36 us -> 52 us  [body(): lax.all_to_all(voltage, ('narrow', 'wide'), split_axis=0, concat_axis=0,...]
    all_to_all x1, waiting for transfers between devices: 39.5 us -> 6.87 us  [body(): lax.all_to_all(intensity, 'wide', split_axis=0, concat_axis=0, tiled=True)]
    all_to_all x1, starting transfers between devices: 10.9 us -> 3.4 us  [body(): lax.all_to_all(intensity, 'wide', split_axis=0, concat_axis=0, tiled=True)]
    ppermute x1, starting transfers between devices: 4.2 us -> 1.91 us  [body(): other = lax.ppermute(by_beam, 'narrow', others)]
    ppermute x1, waiting for transfers between devices: 5.92 us -> 4.48 us  [body(): other = lax.ppermute(by_beam, 'narrow', others)]
    pallas_call x1, Pallas kernels: 10.7 us -> 9.57 us  [beam_power(): pl.pallas_call(functools.partial(beam_kernel, 1.0 / (pols * INTEG)), out_...]
where the time goes in v5:
time: 97.8 us; the launch traced here: 97.5 us
  blocking collectives  52 us (53%)
  Pallas kernels  27.2 us (28%)
  waiting for transfers between devices  11.4 us (12%)
  starting transfers between devices  6.32 us (6%)
    all_to_all x1, blocking collectives, body(): lax.all_to_all(voltage, ('narrow', 'wide'), split_axis=0, concat_axis=0,...  52 us
    pallas_call x1, Pallas kernels, channelize(): pl.pallas_call(functools.partial(channelize_kernel, frames, spectra, tap_...  14.5 us
    pallas_call x1, Pallas kernels, beam_power(): pl.pallas_call(functools.partial(beam_kernel, 1.0 / (pols * INTEG)), out_...  9.57 us
    all_to_all x1, waiting for transfers between devices, body(): lax.all_to_all(intensity, 'wide', split_axis=0, concat_axis=0, tiled=True)  6.87 us
    ppermute x1, waiting for transfers between devices, body(): other = lax.ppermute(by_beam, 'narrow', others)  4.48 us
    all_to_all x1, starting transfers between devices, body(): lax.all_to_all(intensity, 'wide', split_axis=0, concat_axis=0, tiled=True)  3.4 us
  transfers between devices with their start and end apart: 3, of which 2 were waited for; matrix products, arithmetic and copies ran while one was open for 1% of the time, Pallas kernels for 2%

profile of v5, /device:TPU:8, one launch (start us, length us, event | category | flops | bytes accessed | tf_op | source)
XLA Modules:
  0.0 97.5 jit_solution(1012368581123966841)
XLA Ops:
  0.0 14.5 %channelize.1 = bf16[128,2,16,384]{3,2,1,0:T(8,128)(2,1)} custom-call(bf16[12768,128]{1,0:T(8,128)(2,1)} %bitcast.20, f32[16,256]{1,0:T(8,128)} %taps_ref.1, bf16[2,256,768]{2,1,0:T(8,128)(2,1)} %constant.24.clone.table_ref), custom_call_target="tpu_custom_call" | custom-call | tf_op jit(solution)/shard_map/channelize/pallas_call | solution.py:156
  14.5 52.0 %all_to_all.10 = bf16[128,2,2,8,384]{4,3,2,1,0:T(8,128)(2,1)S(1)} all-to-all(bf16[128,2,2,8,384]{4,3,2,1,0:T(8,128)(2,1)} %bitcast.19), channel_id=1, replica_groups=mesh['wide'=8,'narrow'=16] {'narrow','wide'}, dimensions={0} | all-to-all | bytes 6291456 | tf_op jit(solution)/shard_map/all_to_all | solution.py:324
  66.5 0.0 copy-start
  66.5 0.0 copy-start.1
  66.5 9.6 %beam_power.1 = bf16[8,2,48,128]{3,2,1,0:T(8,128)(2,1)} custom-call(bf16[16,8,2,2,8,384]{5,4,3,2,1,0:T(8,128)(2,1)S(1)} %bitcast.15, bf16[2,2,2,512,1024]{4,3,2,1,0:T(8,128)(2,1)} %weight_ref.1), custom_call_target="tpu_custom_call" | custom-call | tf_op jit(solution)/shard_map/beam_power/pallas_call | solution.py:225
  76.1 3.4 %all-to-all-start.1 = ((bf16[8,2,48,128]{3,2,1,0:T(8,128)(2,1)}), bf16[8,2,48,128]{3,2,1,0:T(8,128)(2,1)S(1)}, u32[]{:S(2)}, u32[]{:S(2)}) async-start(bf16[8,2,48,128]{3,2,1,0:T(8,128)(2,1)} %beam_power.1), calls=%async_computation.1 | async-start | bytes 393216 | tf_op jit(solution)/shard_map/all_to_all | solution.py:332
  79.5 6.9 %all-to-all-done.1 = bf16[8,2,48,128]{3,2,1,0:T(8,128)(2,1)S(1)} async-done(((bf16[8,2,48,128]{3,2,1,0:T(8,128)(2,1)}), bf16[8,2,48,128]{3,2,1,0:T(8,128)(2,1)S(1)}, u32[]{:S(2)}, u32[]{:S(2)}) %all-to-all-start.1) | async-done | bytes 196640 | tf_op jit(solution)/shard_map/all_to_all | solution.py:332
  86.3 1.9 %collective-permute-start = (bf16[16,48,128]{2,1,0:T(8,128)(2,1)S(1)}, bf16[16,48,128]{2,1,0:T(8,128)(2,1)S(1)}, u32[]{:S(2)}, u32[]{:S(2)}) collective-permute-start(bf16[16,48,128]{2,1,0:T(8,128)(2,1)S(1)} %bitcast.16), channel_id=1, source_target_pairs={{1,2},{2,1},{3,4},{4,3},{5,6},{6,5},{7,8},{8,7},{9,10},{10,9},{11,... | collective-permute-start | bytes 589832 | tf_op jit(solution)/shard_map/ppermute | solution.py:336
  88.3 1.0 %collective-permute-start.1 = (bf16[16,48,128]{2,1,0:T(8,128)(2,1)S(1)}, bf16[16,48,128]{2,1,0:T(8,128)(2,1)S(1)}, u32[]{:S(2)}, u32[]{:S(2)}) collective-permute-start(bf16[16,48,128]{2,1,0:T(8,128)(2,1)S(1)} %bitcast.17), channel_id=1, source_target_pairs={{0,1},{1,0},{2,3},{3,2},{4,5},{5,4},{6,7},{7,6},{8,9},{9,8},{10,11... | collective-permute-start | bytes 589832 | tf_op jit(solution)/shard_map/ppermute | solution.py:337
  89.3 0.0 copy-done
  89.3 0.0 copy-done.1
  89.3 0.3 convolution_bitcast_fusion
  89.5 0.3 reshape.27
  89.9 1.1 %band.1.matrix_ref = bf16[768,2304]{1,0:T(8,128)(2,1)S(1)} custom-call(s32[1]{0:T(128)} %bitcast.6.odd_ref, f32[48,2304]{1,0:T(8,128)S(1)} %pad.4.row_ref), custom_call_target="tpu_custom_call" | custom-call | tf_op jit(solution)/shard_map/band/pallas_call | solution.py:267
  90.9 0.5 smooth_near.1.part_ref
  91.4 4.5 %collective-permute-done.other_ref = bf16[16,48,128]{2,1,0:T(8,128)(2,1)S(1)} collective-permute-done((bf16[16,48,128]{2,1,0:T(8,128)(2,1)S(1)}, bf16[16,48,128]{2,1,0:T(8,128)(2,1)S(1)}, u32[]{:S(2)}, u32[]{:S(2)}) %collective-permute-start) | collective-permute-done | bytes 196640 | tf_op jit(solution)/shard_map/ppermute | solution.py:336
  95.9 0.0 collective-permute-done.1.pair_ref
  95.9 1.5 %smooth_far.1 = f32[16,48,128]{2,1,0:T(8,128)} custom-call(bf16[16,48,128]{2,1,0:T(8,128)(2,1)S(1)} %collective-permute-done.other_ref, bf16[16,48,128]{2,1,0:T(8,128)(2,1)S(1)} %collective-permute-done.1.pair_ref, f32[768,128]{1,0:T(8,128)S(1)} %smooth_near.1.part_ref, bf16[768,2304]{1,0:T(8,128)(2,1)S(1)} %band.1.matrix_ref), custom_call_target="tpu_custom_call" | custom-call | tf_op jit(solution)/shard_map/smooth_far/pallas_call | solution.py:310
  (1 shorter events, 0.0 us)
Async XLA Ops:
  66.5 22.8 %copy-start = (bf16[33,48,48]{2,0,1:T(8,128)(2,1)S(1)}, bf16[33,48,48]{2,0,1:T(8,128)(2,1)}, u32[]{:S(2)}) copy-start(bf16[33,48,48]{2,0,1:T(8,128)(2,1)} %constant.25.clone) | copy-start | bytes 456196
  66.5 22.8 %copy-start.1 = (f32[33,33]{1,0:T(8,128)S(1)}, f32[33,33]{1,0:T(8,128)}, u32[]{:S(2)}) copy-start(f32[33,33]{1,0:T(8,128)} %param.9) | copy-start | bytes 13072
  76.1 10.3 %all-to-all-start.1 = ((bf16[8,2,48,128]{3,2,1,0:T(8,128)(2,1)}), bf16[8,2,48,128]{3,2,1,0:T(8,128)(2,1)S(1)}, u32[]{:S(2)}, u32[]{:S(2)}) async-start(bf16[8,2,48,128]{3,2,1,0:T(8,128)(2,1)} %beam_power.1), calls=%async_computation.1 | async-start | bytes 393216 | tf_op jit(solution)/shard_map/all_to_all | solution.py:332
  86.3 9.6 %collective-permute-start = (bf16[16,48,128]{2,1,0:T(8,128)(2,1)S(1)}, bf16[16,48,128]{2,1,0:T(8,128)(2,1)S(1)}, u32[]{:S(2)}, u32[]{:S(2)}) collective-permute-start(bf16[16,48,128]{2,1,0:T(8,128)(2,1)S(1)} %bitcast.16), channel_id=1, source_target_pairs={{1,2},{2,1},{3,4},{4,3},{5,6},{6,5},{7,8},{8,7},{9,10},{10,9},{11,... | collective-permute-start | bytes 589832 | tf_op jit(solution)/shard_map/ppermute | solution.py:336
  88.3 7.7 %collective-permute-start.1 = (bf16[16,48,128]{2,1,0:T(8,128)(2,1)S(1)}, bf16[16,48,128]{2,1,0:T(8,128)(2,1)S(1)}, u32[]{:S(2)}, u32[]{:S(2)}) collective-permute-start(bf16[16,48,128]{2,1,0:T(8,128)(2,1)S(1)} %bitcast.17), channel_id=1, source_target_pairs={{0,1},{1,0},{2,3},{3,2},{4,5},{5,4},{6,7},{7,6},{8,9},{9,8},{10,11... | collective-permute-start | bytes 589832 | tf_op jit(solution)/shard_map/ppermute | solution.py:337

commit v6 on v5

--- a/solution.py
+++ b/solution.py
@@ -13,6 +13,10 @@
 HALF = 16
 LANES = 128
 BATCH = 2
+HOIST = 4
+WAITS = ((0,), (1, 2, 3))
+SHORTEST = 4
+PASSES = 3
 
 
 def fourier_table(points, owners):
@@ -28,7 +32,33 @@
     table = table.astype(np.float32)
     high = table.astype(ml_dtypes.bfloat16)
     low = (table - high.astype(np.float32)).astype(ml_dtypes.bfloat16)
-    return np.concatenate([high, high, low], axis=2)
+    return np.concatenate([high, high, low][:PASSES], axis=2)
+
+
+def fast_filter(taps, value):
+    if len(taps) <= SHORTEST:
+
+        def direct(index):
+            total = taps[0] * value(index)
+            for tap in range(1, len(taps)):
+                total = total + taps[tap] * value(index + tap)
+            return total
+
+        return direct
+    even, odd = taps[0::2], taps[1::2]
+    both = [first + second for first, second in zip(even, odd)]
+    early = functools.cache(fast_filter(even, lambda index: value(2 * index)))
+    late = functools.cache(fast_filter(odd, lambda index: value(2 * index + 1)))
+    added = functools.cache(lambda index: value(2 * index + 1) + value(2 * index + 2))
+    mixed = functools.cache(fast_filter(both, added))
+
+    def folded(index):
+        half = index // 2
+        if index % 2 == 0:
+            return early(half) + late(half)
+        return mixed(half) - (early(half + 1) + late(half))
+
+    return folded
 
 
 def channelize_kernel(
@@ -41,8 +71,6 @@
     span = segment * per_frame
     needed = (segment + tap_count - 1) * per_frame
     pitch = lined.shape[0] // group
-    half_taps = tap_count // 2
-    pairs = segment // 2
 
     for member in range(group):
         for lane in range(8):
@@ -55,40 +83,15 @@
         half = part // 2
         columns = slice(half * LANES, (half + 1) * LANES)
         taps = [jnp.broadcast_to(taps_ref[t : t + 1, columns], (8, LANES)) for t in range(tap_count)]
-        even, odd = taps[0::2], taps[1::2]
-        both = [first + second for first, second in zip(even, odd)]
 
         def frame(index):
             start = member * pitch + (per_frame * index + part) * 8
             return lined[start : start + 8, :]
 
-        def put(index, values):
+        filtered = fast_filter(taps, frame)
+        for index in range(segment):
             row = member * spectra + index * 8
-            windowed[row : row + 8, part * LANES : (part + 1) * LANES] = values
-
-        def feed(totals, factors, values, index, count):
-            for tap in range(half_taps):
-                target = index - tap
-                if 0 <= target < count:
-                    term = factors[tap] * values
-                    totals[target] = totals[target] + term if target in totals else term
-
-        evens, odds, sums = {}, {}, {}
-        late = None
-        for index in range(pairs + half_taps):
-            early = frame(2 * index)
-            feed(evens, even, early, index, pairs + 1)
-            if index > 0:
-                feed(odds, odd, late, index - 1, pairs)
-                feed(sums, both, late + early, index - 1, pairs)
-                done = index - half_taps
-                if done >= 0:
-                    second = odds.pop(done)
-                    put(2 * done, evens[done] + second)
-                    put(2 * done + 1, sums.pop(done) - (evens[done + 1] + second))
-                    evens.pop(done)
-            if index < pairs + half_taps - 1:
-                late = frame(2 * index + 1)
+            windowed[row : row + 8, part * LANES : (part + 1) * LANES] = filtered(index)
 
     contract = (((1,), (1,)), ((), ()))
     parities, outputs, points = table_ref.shape[0], table_ref.shape[1], windowed.shape[1]
@@ -107,7 +110,7 @@
             low = (folded - high.astype(jnp.float32)).astype(jnp.bfloat16)
             spectrum = lax.dot_general(
                 table_ref[parity],
-                jnp.concatenate([high, low, high], axis=1),
+                jnp.concatenate([high, low, high][:PASSES], axis=1),
                 contract,
                 preferred_element_type=jnp.float32,
             )
@@ -190,22 +193,30 @@
         ]
         return jnp.concatenate(blocks, axis=0).T
 
-    copies = {}
-    for channel in range(per_device):
-        for pol in range(pols):
-            copies[channel, pol] = pltpu.make_async_copy(
-                weight_ref.at[channel, pol], held.at[channel, pol], arrived.at[channel, pol]
-            )
-            copies[channel, pol].start()
+    stages = [(channel, pol) for channel in range(per_device) for pol in range(pols)]
+    copies = [
+        pltpu.make_async_copy(weight_ref.at[stage], held.at[stage], arrived.at[stage]) for stage in stages
+    ]
+    for copy in copies:
+        copy.start()
+
+    def left_side(channel, pol):
+        real = gathered(channel, pol, 0)
+        imag = gathered(channel, pol, 1)
+        return jnp.concatenate(
+            [jnp.concatenate([real, -imag], axis=1), jnp.concatenate([imag, real], axis=1)], axis=0
+        )
+
+    ready = [left_side(*stage) for stage in stages[:HOIST]]
     for channel in range(per_device):
         total = None
         for pol in range(pols):
-            real = gathered(channel, pol, 0)
-            imag = gathered(channel, pol, 1)
-            lhs = jnp.concatenate(
-                [jnp.concatenate([real, -imag], axis=1), jnp.concatenate([imag, real], axis=1)], axis=0
-            )
-            copies[channel, pol].wait()
+            index = channel * pols + pol
+            for group in WAITS:
+                if group[0] == index:
+                    for member in group:
+                        copies[member].wait()
+            lhs = ready[index] if index < HOIST else left_side(channel, pol)
             weights = held[channel, pol].reshape(2 * dishes, beams)
             formed = jnp.dot(lhs, weights, preferred_element_type=jnp.float32)
             power = formed * formed

time: 97.8 us -> 96.6 us (0.988)
  Pallas kernels: 27.2 us -> 26 us
where the time goes in v6:
time: 96.6 us; the launch traced here: 96.3 us
  blocking collectives  52 us (54%)
  Pallas kernels  26 us (27%)
  waiting for transfers between devices  11.4 us (12%)
  starting transfers between devices  6.31 us (7%)
    all_to_all x1, blocking collectives, body(): lax.all_to_all(voltage, ('narrow', 'wide'), split_axis=0, concat_axis=0,...  52 us
    pallas_call x1, Pallas kernels, channelize(): pl.pallas_call(functools.partial(channelize_kernel, frames, spectra, tap_...  13.6 us
    pallas_call x1, Pallas kernels, beam_power(): pl.pallas_call(functools.partial(beam_kernel, 1.0 / (pols * INTEG)), out_...  9.3 us
    all_to_all x1, waiting for transfers between devices, body(): lax.all_to_all(intensity, 'wide', split_axis=0, concat_axis=0, tiled=True)  6.87 us
    ppermute x1, waiting for transfers between devices, body(): other = lax.ppermute(by_beam, 'narrow', others)  4.48 us
    all_to_all x1, starting transfers between devices, body(): lax.all_to_all(intensity, 'wide', split_axis=0, concat_axis=0, tiled=True)  3.4 us
  transfers between devices with their start and end apart: 3, of which 2 were waited for; matrix products, arithmetic and copies ran while one was open for 1% of the time, Pallas kernels for 2%

profile of v6, /device:TPU:8, one launch (start us, length us, event | category | flops | bytes accessed | tf_op | source)
XLA Modules:
  0.0 96.3 jit_solution(11188880240803975478)
XLA Ops:
  0.0 13.6 %channelize.1 = bf16[128,2,16,384]{3,2,1,0:T(8,128)(2,1)} custom-call(bf16[12768,128]{1,0:T(8,128)(2,1)} %bitcast.20, f32[16,256]{1,0:T(8,128)} %taps_ref.1, bf16[2,256,768]{2,1,0:T(8,128)(2,1)} %constant.24.clone.table_ref), custom_call_target="tpu_custom_call" | custom-call | tf_op jit(solution)/shard_map/channelize/pallas_call | solution.py:159
  13.6 52.0 %all_to_all.10 = bf16[128,2,2,8,384]{4,3,2,1,0:T(8,128)(2,1)S(1)} all-to-all(bf16[128,2,2,8,384]{4,3,2,1,0:T(8,128)(2,1)} %bitcast.19), channel_id=1, replica_groups=mesh['wide'=8,'narrow'=16] {'narrow','wide'}, dimensions={0} | all-to-all | bytes 6291456 | tf_op jit(solution)/shard_map/all_to_all | solution.py:335
  65.6 0.0 copy-start
  65.6 0.0 copy-start.1
  65.6 9.3 %beam_power.1 = bf16[8,2,48,128]{3,2,1,0:T(8,128)(2,1)} custom-call(bf16[16,8,2,2,8,384]{5,4,3,2,1,0:T(8,128)(2,1)S(1)} %bitcast.15, bf16[2,2,2,512,1024]{4,3,2,1,0:T(8,128)(2,1)} %weight_ref.1), custom_call_target="tpu_custom_call" | custom-call | tf_op jit(solution)/shard_map/beam_power/pallas_call | solution.py:236
  74.9 3.4 %all-to-all-start.1 = ((bf16[8,2,48,128]{3,2,1,0:T(8,128)(2,1)}), bf16[8,2,48,128]{3,2,1,0:T(8,128)(2,1)S(1)}, u32[]{:S(2)}, u32[]{:S(2)}) async-start(bf16[8,2,48,128]{3,2,1,0:T(8,128)(2,1)} %beam_power.1), calls=%async_computation.1 | async-start | bytes 393216 | tf_op jit(solution)/shard_map/all_to_all | solution.py:343
  78.3 6.9 %all-to-all-done.1 = bf16[8,2,48,128]{3,2,1,0:T(8,128)(2,1)S(1)} async-done(((bf16[8,2,48,128]{3,2,1,0:T(8,128)(2,1)}), bf16[8,2,48,128]{3,2,1,0:T(8,128)(2,1)S(1)}, u32[]{:S(2)}, u32[]{:S(2)}) %all-to-all-start.1) | async-done | bytes 196640 | tf_op jit(solution)/shard_map/all_to_all | solution.py:343
  85.2 1.9 %collective-permute-start = (bf16[16,48,128]{2,1,0:T(8,128)(2,1)S(1)}, bf16[16,48,128]{2,1,0:T(8,128)(2,1)S(1)}, u32[]{:S(2)}, u32[]{:S(2)}) collective-permute-start(bf16[16,48,128]{2,1,0:T(8,128)(2,1)S(1)} %bitcast.16), channel_id=1, source_target_pairs={{1,2},{2,1},{3,4},{4,3},{5,6},{6,5},{7,8},{8,7},{9,10},{10,9},{11,... | collective-permute-start | bytes 589832 | tf_op jit(solution)/shard_map/ppermute | solution.py:347
  87.1 1.0 %collective-permute-start.1 = (bf16[16,48,128]{2,1,0:T(8,128)(2,1)S(1)}, bf16[16,48,128]{2,1,0:T(8,128)(2,1)S(1)}, u32[]{:S(2)}, u32[]{:S(2)}) collective-permute-start(bf16[16,48,128]{2,1,0:T(8,128)(2,1)S(1)} %bitcast.17), channel_id=1, source_target_pairs={{0,1},{1,0},{2,3},{3,2},{4,5},{5,4},{6,7},{7,6},{8,9},{9,8},{10,11... | collective-permute-start | bytes 589832 | tf_op jit(solution)/shard_map/ppermute | solution.py:348
  88.1 0.0 copy-done
  88.1 0.0 copy-done.1
  88.1 0.3 convolution_bitcast_fusion
  88.4 0.3 reshape.27
  88.7 1.1 %band.1.matrix_ref = bf16[768,2304]{1,0:T(8,128)(2,1)S(1)} custom-call(s32[1]{0:T(128)} %bitcast.6.odd_ref, f32[48,2304]{1,0:T(8,128)S(1)} %pad.4.row_ref), custom_call_target="tpu_custom_call" | custom-call | tf_op jit(solution)/shard_map/band/pallas_call | solution.py:278
  89.8 0.5 smooth_near.1.part_ref
  90.3 4.5 %collective-permute-done.other_ref = bf16[16,48,128]{2,1,0:T(8,128)(2,1)S(1)} collective-permute-done((bf16[16,48,128]{2,1,0:T(8,128)(2,1)S(1)}, bf16[16,48,128]{2,1,0:T(8,128)(2,1)S(1)}, u32[]{:S(2)}, u32[]{:S(2)}) %collective-permute-start) | collective-permute-done | bytes 196640 | tf_op jit(solution)/shard_map/ppermute | solution.py:347
  94.8 0.0 collective-permute-done.1.pair_ref
  94.8 1.6 %smooth_far.1 = f32[16,48,128]{2,1,0:T(8,128)} custom-call(bf16[16,48,128]{2,1,0:T(8,128)(2,1)S(1)} %collective-permute-done.other_ref, bf16[16,48,128]{2,1,0:T(8,128)(2,1)S(1)} %collective-permute-done.1.pair_ref, f32[768,128]{1,0:T(8,128)S(1)} %smooth_near.1.part_ref, bf16[768,2304]{1,0:T(8,128)(2,1)S(1)} %band.1.matrix_ref), custom_call_target="tpu_custom_call" | custom-call | tf_op jit(solution)/shard_map/smooth_far/pallas_call | solution.py:321
  (1 shorter events, 0.0 us)
Async XLA Ops:
  65.6 22.5 %copy-start = (bf16[33,48,48]{2,0,1:T(8,128)(2,1)S(1)}, bf16[33,48,48]{2,0,1:T(8,128)(2,1)}, u32[]{:S(2)}) copy-start(bf16[33,48,48]{2,0,1:T(8,128)(2,1)} %constant.25.clone) | copy-start | bytes 456196
  65.6 22.5 %copy-start.1 = (f32[33,33]{1,0:T(8,128)S(1)}, f32[33,33]{1,0:T(8,128)}, u32[]{:S(2)}) copy-start(f32[33,33]{1,0:T(8,128)} %param.9) | copy-start | bytes 13072
  74.9 10.3 %all-to-all-start.1 = ((bf16[8,2,48,128]{3,2,1,0:T(8,128)(2,1)}), bf16[8,2,48,128]{3,2,1,0:T(8,128)(2,1)S(1)}, u32[]{:S(2)}, u32[]{:S(2)}) async-start(bf16[8,2,48,128]{3,2,1,0:T(8,128)(2,1)} %beam_power.1), calls=%async_computation.1 | async-start | bytes 393216 | tf_op jit(solution)/shard_map/all_to_all | solution.py:343
  85.2 9.6 %collective-permute-start = (bf16[16,48,128]{2,1,0:T(8,128)(2,1)S(1)}, bf16[16,48,128]{2,1,0:T(8,128)(2,1)S(1)}, u32[]{:S(2)}, u32[]{:S(2)}) collective-permute-start(bf16[16,48,128]{2,1,0:T(8,128)(2,1)S(1)} %bitcast.16), channel_id=1, source_target_pairs={{1,2},{2,1},{3,4},{4,3},{5,6},{6,5},{7,8},{8,7},{9,10},{10,9},{11,... | collective-permute-start | bytes 589832 | tf_op jit(solution)/shard_map/ppermute | solution.py:347
  87.1 7.7 %collective-permute-start.1 = (bf16[16,48,128]{2,1,0:T(8,128)(2,1)S(1)}, bf16[16,48,128]{2,1,0:T(8,128)(2,1)S(1)}, u32[]{:S(2)}, u32[]{:S(2)}) collective-permute-start(bf16[16,48,128]{2,1,0:T(8,128)(2,1)S(1)} %bitcast.17), channel_id=1, source_target_pairs={{0,1},{1,0},{2,3},{3,2},{4,5},{5,4},{6,7},{7,6},{8,9},{9,8},{10,11... | collective-permute-start | bytes 589832 | tf_op jit(solution)/shard_map/ppermute | solution.py:348

commit v7 on v6

--- a/solution.py
+++ b/solution.py
@@ -171,7 +171,7 @@
             pltpu.VMEM((group * spectra, 2 * points), jnp.float32),
             pltpu.VMEM((spectra // LANES, 2 * points * inputs_here, LANES), jnp.float32),
             pltpu.VMEM(shape, jnp.bfloat16),
-            pltpu.SemaphoreType.DMA((4,)),
+            pltpu.SemaphoreType.DMA((8,)),
         ],
         compiler_params=pltpu.CompilerParams(vmem_limit_bytes=60 << 20),
         name="channelize",

time: 96.6 us -> 96.6 us (level)
  no operation moved by 1% of the time
where the time goes in v7:
time: 96.6 us; the launch traced here: 96.3 us
  blocking collectives  52 us (54%)
  Pallas kernels  26 us (27%)
  waiting for transfers between devices  11.4 us (12%)
  starting transfers between devices  6.31 us (7%)
    all_to_all x1, blocking collectives, body(): lax.all_to_all(voltage, ('narrow', 'wide'), split_axis=0, concat_axis=0,...  52 us
    pallas_call x1, Pallas kernels, channelize(): pl.pallas_call(functools.partial(channelize_kernel, frames, spectra, tap_...  13.6 us
    pallas_call x1, Pallas kernels, beam_power(): pl.pallas_call(functools.partial(beam_kernel, 1.0 / (pols * INTEG)), out_...  9.3 us
    all_to_all x1, waiting for transfers between devices, body(): lax.all_to_all(intensity, 'wide', split_axis=0, concat_axis=0, tiled=True)  6.87 us
    ppermute x1, waiting for transfers between devices, body(): other = lax.ppermute(by_beam, 'narrow', others)  4.48 us
    all_to_all x1, starting transfers between devices, body(): lax.all_to_all(intensity, 'wide', split_axis=0, concat_axis=0, tiled=True)  3.4 us
  transfers between devices with their start and end apart: 3, of which 2 were waited for; matrix products, arithmetic and copies ran while one was open for 1% of the time, Pallas kernels for 2%

profile of v7, /device:TPU:8, one launch (start us, length us, event | category | flops | bytes accessed | tf_op | source)
XLA Modules:
  0.0 96.3 jit_solution(7616346415500084938)
XLA Ops:
  0.0 13.6 %channelize.1 = bf16[128,2,16,384]{3,2,1,0:T(8,128)(2,1)} custom-call(bf16[12768,128]{1,0:T(8,128)(2,1)} %bitcast.20, f32[16,256]{1,0:T(8,128)} %taps_ref.1, bf16[2,256,768]{2,1,0:T(8,128)(2,1)} %constant.24.clone.table_ref), custom_call_target="tpu_custom_call" | custom-call | tf_op jit(solution)/shard_map/channelize/pallas_call | solution.py:159
  13.6 52.0 %all_to_all.10 = bf16[128,2,2,8,384]{4,3,2,1,0:T(8,128)(2,1)S(1)} all-to-all(bf16[128,2,2,8,384]{4,3,2,1,0:T(8,128)(2,1)} %bitcast.19), channel_id=1, replica_groups=mesh['wide'=8,'narrow'=16] {'narrow','wide'}, dimensions={0} | all-to-all | bytes 6291456 | tf_op jit(solution)/shard_map/all_to_all | solution.py:335
  65.6 0.0 copy-start
  65.6 0.0 copy-start.1
  65.6 9.3 %beam_power.1 = bf16[8,2,48,128]{3,2,1,0:T(8,128)(2,1)} custom-call(bf16[16,8,2,2,8,384]{5,4,3,2,1,0:T(8,128)(2,1)S(1)} %bitcast.15, bf16[2,2,2,512,1024]{4,3,2,1,0:T(8,128)(2,1)} %weight_ref.1), custom_call_target="tpu_custom_call" | custom-call | tf_op jit(solution)/shard_map/beam_power/pallas_call | solution.py:236
  74.9 3.4 %all-to-all-start.1 = ((bf16[8,2,48,128]{3,2,1,0:T(8,128)(2,1)}), bf16[8,2,48,128]{3,2,1,0:T(8,128)(2,1)S(1)}, u32[]{:S(2)}, u32[]{:S(2)}) async-start(bf16[8,2,48,128]{3,2,1,0:T(8,128)(2,1)} %beam_power.1), calls=%async_computation.1 | async-start | bytes 393216 | tf_op jit(solution)/shard_map/all_to_all | solution.py:343
  78.3 6.9 %all-to-all-done.1 = bf16[8,2,48,128]{3,2,1,0:T(8,128)(2,1)S(1)} async-done(((bf16[8,2,48,128]{3,2,1,0:T(8,128)(2,1)}), bf16[8,2,48,128]{3,2,1,0:T(8,128)(2,1)S(1)}, u32[]{:S(2)}, u32[]{:S(2)}) %all-to-all-start.1) | async-done | bytes 196640 | tf_op jit(solution)/shard_map/all_to_all | solution.py:343
  85.2 1.9 %collective-permute-start = (bf16[16,48,128]{2,1,0:T(8,128)(2,1)S(1)}, bf16[16,48,128]{2,1,0:T(8,128)(2,1)S(1)}, u32[]{:S(2)}, u32[]{:S(2)}) collective-permute-start(bf16[16,48,128]{2,1,0:T(8,128)(2,1)S(1)} %bitcast.16), channel_id=1, source_target_pairs={{1,2},{2,1},{3,4},{4,3},{5,6},{6,5},{7,8},{8,7},{9,10},{10,9},{11,... | collective-permute-start | bytes 589832 | tf_op jit(solution)/shard_map/ppermute | solution.py:347
  87.1 1.0 %collective-permute-start.1 = (bf16[16,48,128]{2,1,0:T(8,128)(2,1)S(1)}, bf16[16,48,128]{2,1,0:T(8,128)(2,1)S(1)}, u32[]{:S(2)}, u32[]{:S(2)}) collective-permute-start(bf16[16,48,128]{2,1,0:T(8,128)(2,1)S(1)} %bitcast.17), channel_id=1, source_target_pairs={{0,1},{1,0},{2,3},{3,2},{4,5},{5,4},{6,7},{7,6},{8,9},{9,8},{10,11... | collective-permute-start | bytes 589832 | tf_op jit(solution)/shard_map/ppermute | solution.py:348
  88.1 0.0 copy-done
  88.1 0.0 copy-done.1
  88.1 0.3 convolution_bitcast_fusion
  88.4 0.3 reshape.27
  88.7 1.1 %band.1.matrix_ref = bf16[768,2304]{1,0:T(8,128)(2,1)S(1)} custom-call(s32[1]{0:T(128)} %bitcast.6.odd_ref, f32[48,2304]{1,0:T(8,128)S(1)} %pad.4.row_ref), custom_call_target="tpu_custom_call" | custom-call | tf_op jit(solution)/shard_map/band/pallas_call | solution.py:278
  89.8 0.5 smooth_near.1.part_ref
  90.3 4.5 %collective-permute-done.other_ref = bf16[16,48,128]{2,1,0:T(8,128)(2,1)S(1)} collective-permute-done((bf16[16,48,128]{2,1,0:T(8,128)(2,1)S(1)}, bf16[16,48,128]{2,1,0:T(8,128)(2,1)S(1)}, u32[]{:S(2)}, u32[]{:S(2)}) %collective-permute-start) | collective-permute-done | bytes 196640 | tf_op jit(solution)/shard_map/ppermute | solution.py:347
  94.8 0.0 collective-permute-done.1.pair_ref
  94.8 1.6 %smooth_far.1 = f32[16,48,128]{2,1,0:T(8,128)} custom-call(bf16[16,48,128]{2,1,0:T(8,128)(2,1)S(1)} %collective-permute-done.other_ref, bf16[16,48,128]{2,1,0:T(8,128)(2,1)S(1)} %collective-permute-done.1.pair_ref, f32[768,128]{1,0:T(8,128)S(1)} %smooth_near.1.part_ref, bf16[768,2304]{1,0:T(8,128)(2,1)S(1)} %band.1.matrix_ref), custom_call_target="tpu_custom_call" | custom-call | tf_op jit(solution)/shard_map/smooth_far/pallas_call | solution.py:321
  (1 shorter events, 0.0 us)
Async XLA Ops:
  65.6 22.5 %copy-start = (bf16[33,48,48]{2,0,1:T(8,128)(2,1)S(1)}, bf16[33,48,48]{2,0,1:T(8,128)(2,1)}, u32[]{:S(2)}) copy-start(bf16[33,48,48]{2,0,1:T(8,128)(2,1)} %constant.25.clone) | copy-start | bytes 456196
  65.6 22.5 %copy-start.1 = (f32[33,33]{1,0:T(8,128)S(1)}, f32[33,33]{1,0:T(8,128)}, u32[]{:S(2)}) copy-start(f32[33,33]{1,0:T(8,128)} %param.9) | copy-start | bytes 13072
  74.9 10.3 %all-to-all-start.1 = ((bf16[8,2,48,128]{3,2,1,0:T(8,128)(2,1)}), bf16[8,2,48,128]{3,2,1,0:T(8,128)(2,1)S(1)}, u32[]{:S(2)}, u32[]{:S(2)}) async-start(bf16[8,2,48,128]{3,2,1,0:T(8,128)(2,1)} %beam_power.1), calls=%async_computation.1 | async-start | bytes 393216 | tf_op jit(solution)/shard_map/all_to_all | solution.py:343
  85.2 9.6 %collective-permute-start = (bf16[16,48,128]{2,1,0:T(8,128)(2,1)S(1)}, bf16[16,48,128]{2,1,0:T(8,128)(2,1)S(1)}, u32[]{:S(2)}, u32[]{:S(2)}) collective-permute-start(bf16[16,48,128]{2,1,0:T(8,128)(2,1)S(1)} %bitcast.16), channel_id=1, source_target_pairs={{1,2},{2,1},{3,4},{4,3},{5,6},{6,5},{7,8},{8,7},{9,10},{10,9},{11,... | collective-permute-start | bytes 589832 | tf_op jit(solution)/shard_map/ppermute | solution.py:347
  87.1 7.7 %collective-permute-start.1 = (bf16[16,48,128]{2,1,0:T(8,128)(2,1)S(1)}, bf16[16,48,128]{2,1,0:T(8,128)(2,1)S(1)}, u32[]{:S(2)}, u32[]{:S(2)}) collective-permute-start(bf16[16,48,128]{2,1,0:T(8,128)(2,1)S(1)} %bitcast.17), channel_id=1, source_target_pairs={{0,1},{1,0},{2,3},{3,2},{4,5},{5,4},{6,7},{7,6},{8,9},{9,8},{10,11... | collective-permute-start | bytes 589832 | tf_op jit(solution)/shard_map/ppermute | solution.py:348
